TPU v7x, 512 devices: a whole 4x4x16 slice. The times are simulated.
512 devices in a mesh: dp: 8 (over x, core), expert: 64 (over y, z).
Axes of the slice: x: 4, y: 4, z: 16, core: 2. Of those that a mesh axis runs over, the one named last changes fastest.
Arguments:
- head_outputs: bfloat16 [65536, 8, 128], P(('dp', 'expert')), may hold values from -6 to 6
- out_grad: bfloat16 [65536, 4096], P(('dp', 'expert')), may hold values from -0.29882812 to 0.29882812
- gate_weights: bfloat16 [65536, 8], P(('dp', 'expert')), may hold values from 0.099609375 to 1
- route_ids: int32 [65536, 8], P(('dp', 'expert')), may hold values from 0 to 63, all different within a row; in each aligned block of 128 rows (0 to 127, 128 to 255, ...) at most 18 rows name the same one
- out_proj: bfloat16 [64, 128, 4096], P('expert'), may hold values from -0.5 to 0.5
Outputs:
- grad_head: bfloat16 [65536, 8, 128], P(('dp', 'expert'))
- grad_gate: bfloat16 [65536, 8], P(('dp', 'expert'))
- grad_proj: float32 [64, 128, 4096], P('expert', 'dp')
Inputs may be any that keep to these rules, and one draw needn't show every extreme that they name: `route_ids`: each row names 8 different head experts. Within the 128 rows of one device no head expert is named by more than 18 rows, and in some devices' rows one is named by exactly 18.
All inputs are finite; a program needn't handle non-finite values.
Results may differ from a plain program's by a relative error of at most 0.0049.
Values may be sent and summed in bfloat16 or wider, within the bound.
A program may use at most 128 MiB of HBM per device.

v0:
```python
import jax
import jax.numpy as jnp
from jax import lax
from jax.sharding import PartitionSpec as P

soft_cap = 1.5


def block_rows(row_total):
    for block_size in (512, 384, 256, 128):
        if row_total % block_size == 0:
            return block_size
    return row_total


def owner_work(received_grad, received_head, received_gate, weights):
    row_count, slot_width, features = received_grad.shape
    local_experts, head_dim, _ = weights.shape
    sources = row_count // local_experts
    grad_all = received_grad.reshape(sources, local_experts, slot_width, features)
    head_all = received_head.reshape(sources, local_experts, slot_width, head_dim)
    gate_all = received_gate.reshape(sources, local_experts, slot_width)
    heads_back, gates_back, weight_sums = ([], [], [])
    row_total = sources * slot_width
    block_size = block_rows(row_total)
    blocks = row_total // block_size
    grad_rows = grad_all[:, 0].reshape(row_total, features)
    head_rows = head_all[:, 0].reshape(row_total, head_dim)
    gate_rows = gate_all[:, 0].reshape(row_total)
    weight = weights[0]

    def advance(
        index,
        carry,
        grad_rows=grad_rows,
        head_rows=head_rows,
        gate_rows=gate_rows,
        weight=weight,
        block_size=block_size,
    ):
        running, head_out, gate_out = carry
        start_row = index * block_size
        grad_block = lax.dynamic_slice_in_dim(grad_rows, start_row, block_size, 0)
        head_block = lax.dynamic_slice_in_dim(head_rows, start_row, block_size, 0)
        gate_block = lax.dynamic_slice_in_dim(gate_rows, start_row, block_size, 0)
        pre_cap = jnp.dot(head_block, weight, preferred_element_type=jnp.float32)
        capped = jnp.tanh(pre_cap / soft_cap)
        grad_pre = (
            gate_block[:, None].astype(jnp.float32)
            * grad_block.astype(jnp.float32)
            * (1.0 - capped * capped)
        ).astype(jnp.bfloat16)
        head_grad = lax.dot_general(
            grad_pre, weight, (((1,), (1,)), ((), ())), preferred_element_type=jnp.float32
        ).astype(jnp.bfloat16)
        gate_grad = jnp.sum(grad_block.astype(jnp.float32) * (soft_cap * capped), axis=1).astype(
            jnp.bfloat16
        )
        running = running + lax.dot_general(
            head_block, grad_pre, (((0,), (0,)), ((), ())), preferred_element_type=jnp.float32
        )
        head_out = lax.dynamic_update_slice_in_dim(head_out, head_grad, start_row, 0)
        gate_out = lax.dynamic_update_slice_in_dim(gate_out, gate_grad, start_row, 0)
        return (running, head_out, gate_out)

    start_carry = (
        jnp.zeros((head_dim, features), jnp.float32),
        jnp.zeros((row_total, head_dim), jnp.bfloat16),
        jnp.zeros((row_total,), jnp.bfloat16),
    )
    weight_sum, head_grad, gate_grad = lax.fori_loop(0, blocks, advance, start_carry)
    heads_back.append(head_grad.reshape(sources, slot_width, head_dim))
    gates_back.append(gate_grad.reshape(sources, slot_width))
    weight_sums.append(weight_sum)
    back_head = jnp.stack(heads_back, axis=1).reshape(row_count, slot_width, head_dim)
    back_gate = jnp.stack(gates_back, axis=1).reshape(row_count, slot_width)
    return (back_head, back_gate, jnp.stack(weight_sums))


def local(head_outputs, out_grad, gate_weights, route_ids, out_proj):
    tok_rows, top_count, head_dim = head_outputs.shape
    features = out_grad.shape[1]
    local_experts = out_proj.shape[0]
    experts = local_experts * lax.axis_size("expert")
    capacity = 9 * tok_rows * top_count // (8 * experts)
    pair_count = tok_rows * top_count
    flat_routes = route_ids.reshape(pair_count)
    one_hot = (flat_routes[:, None] == jnp.arange(experts, dtype=jnp.int32)[None, :]).astype(
        jnp.int32
    )
    before = jnp.cumsum(one_hot, axis=0) - one_hot
    position = jnp.sum(before * one_hot, axis=1)
    target = flat_routes * capacity + position
    source = (
        jnp.full((experts * capacity,), pair_count, jnp.int32)
        .at[target]
        .set(jnp.arange(pair_count, dtype=jnp.int32))
    )
    send_grad = jnp.take(out_grad, source // top_count, axis=0, mode="fill", fill_value=0).reshape(
        experts, capacity, features
    )
    send_head = jnp.take(
        head_outputs.reshape(pair_count, head_dim), source, axis=0, mode="fill", fill_value=0
    ).reshape(experts, capacity, head_dim)
    send_gate = jnp.take(
        gate_weights.reshape(pair_count), source, axis=0, mode="fill", fill_value=0
    ).reshape(experts, capacity)
    received = (
        lax.all_to_all(send_grad, "expert", split_axis=0, concat_axis=0, tiled=True),
        lax.all_to_all(send_head, "expert", split_axis=0, concat_axis=0, tiled=True),
        lax.all_to_all(send_gate, "expert", split_axis=0, concat_axis=0, tiled=True),
    )
    back_head, back_gate, weight_sum = owner_work(received[0], received[1], received[2], out_proj)
    got_head, got_gate = (
        lax.all_to_all(back_head, "expert", split_axis=0, concat_axis=0, tiled=True),
        lax.all_to_all(back_gate, "expert", split_axis=0, concat_axis=0, tiled=True),
    )
    grad_head = jnp.take(got_head.reshape(experts * capacity, head_dim), target, axis=0).reshape(
        tok_rows, top_count, head_dim
    )
    grad_gate = jnp.take(got_gate.reshape(experts * capacity), target, axis=0).reshape(
        tok_rows, top_count
    )
    proj_parts = [lax.psum_scatter(weight_sum[0], "dp", scatter_dimension=0, tiled=True)]
    return (grad_head, grad_gate, jnp.stack(proj_parts))


def solution(mesh):
    return jax.shard_map(
        local,
        mesh=mesh,
        in_specs=(
            P(("dp", "expert"), None, None),
            P(("dp", "expert"), None),
            P(("dp", "expert"), None),
            P(("dp", "expert"), None),
            P("expert", None, None),
        ),
        out_specs=(
            P(("dp", "expert"), None, None),
            P(("dp", "expert"), None),
            P("expert", "dp", None),
        ),
        check_vma=False,
    )
```

profile of v0, /device:TPU:6, one launch (start us, length us, event | category | flops | bytes accessed | tf_op | source)
XLA Modules:
  0.0 788.8 jit_solution(5179374057815660955)
XLA Ops:
  7.2 0.9 copy.16
  8.3 18.0 %reduce-window.6 = s32[64,8,128]{2,1,0:T(8,128)S(1)} reduce-window(s32[64,8,128]{2,1,0:T(8,128)S(1)} %fusion.11, s32[]{:T(128)} %constant.134.clone.1), window={size=1x1x128 pad=0_0x0_0x127_0}, to_apply=%region_0.0 | reduce-window | flops 8323072 | bytes 524292 | tf_op jit(solution)/shard_map/reduce-window
  26.4 0.1 copy.19
  26.7 0.1 broadcast_add_fusion
  27.1 4.3 scatter_custom_fusion
  31.4 0.8 copy.21
  32.3 7.3 gather_fusion.1
  39.6 0.8 select_n.94
  40.4 18.7 %all-to-all-start.1 = ((bf16[64,1,18]{2,1,0:T(2,128)(2,1)}), bf16[64,1,18]{2,1,0:T(2,128)(2,1)S(1)}, u32[]{:S(2)}, u32[]{:S(2)}) async-start(bf16[64,1,18]{2,1,0:T(2,128)(2,1)} %select_n.94), calls=%async_computation.1 | async-start | bytes 65536 | tf_op jit(solution)/shard_map/all_to_all | solution.py:111
  59.2 0.1 broadcast_in_dim.70
  59.3 2.9 gather_fusion
  62.4 1.0 broadcast_select_fusion.1
  63.4 8.0 %gather_fusion.2 = bf16[1152,4096]{1,0:T(8,128)(2,1)} fusion(bf16[128,4096]{1,0:T(8,128)(2,1)S(1)} %copy-done, s32[2048]{0:T(1024)S(1)} %pad_clamp_fusion), kind=kCustom, calls=%fused_computation.2 | custom fusion | bytes 18878976 | tf_op jit(solution)/shard_map/jit(_take)/gather | solution.py:99
  71.4 13.9 %gather.32 = bf16[64,18,4096]{2,1,0:T(8,128)(2,1)} reshape(bf16[1152,4096]{1,0:T(8,128)(2,1)} %gather_fusion.2) | data formatting | bytes 18874368 | tf_op jit(solution)/shard_map/jit(_take)/gather | solution.py:99
  85.3 0.1 broadcast_in_dim.74
  85.5 15.1 %all-to-all-start = ((bf16[64,18,128]{2,1,0:T(8,128)(2,1)}), bf16[64,18,128]{2,1,0:T(8,128)(2,1)S(1)}, u32[]{:S(2)}, u32[]{:S(2)}) async-start(bf16[64,18,128]{2,1,0:T(8,128)(2,1)} %broadcast_select_fusion.1), calls=%async_computation | async-start | bytes 786432 | tf_op jit(solution)/shard_map/all_to_all | solution.py:110
  100.6 10.7 %broadcast_select_fusion = bf16[64,18,4096]{2,1,0:T(8,128)(2,1)} fusion(bf16[64,18,4096]{2,1,0:T(8,128)(2,1)} %gather.32, pred[64,18]{1,0:T(8,128)(4,1)S(1)} %broadcast_in_dim.74), kind=kLoop, calls=%fused_computation.20 | loop fusion | flops 4718592 | bytes 18875520 | tf_op jit(solution)/shard_map/jit(_take)/select_n | solution.py:99
  111.3 15.1 %all-to-all-done = bf16[64,18,128]{2,1,0:T(8,128)(2,1)S(1)} async-done(((bf16[64,18,128]{2,1,0:T(8,128)(2,1)}), bf16[64,18,128]{2,1,0:T(8,128)(2,1)S(1)}, u32[]{:S(2)}, u32[]{:S(2)}) %all-to-all-start) | async-done | bytes 294944 | tf_op jit(solution)/shard_map/all_to_all | solution.py:110
  126.4 6.9 all-to-all-start.2
  133.3 0.2 reduce-scatter.2.cloned.1.call-start
  133.6 0.1 reshape_squeeze_reshape.10
  133.9 545.3 %all-to-all-done.2 = bf16[64,18,4096]{2,1,0:T(8,128)(2,1)} async-done(((bf16[64,18,4096]{2,1,0:T(8,128)(2,1)}), bf16[64,18,4096]{2,1,0:T(8,128)(2,1)}, u32[]{:S(2)}, u32[]{:S(2)}) %all-to-all-start.2) | async-done | bytes 9437216 | tf_op jit(solution)/shard_map/all_to_all | solution.py:109
  679.2 14.1 %reshape_squeeze_reshape.11 = bf16[1152,4096]{1,0:T(8,128)(2,1)} reshape(bf16[64,18,4096]{2,1,0:T(8,128)(2,1)} %all-to-all-done.2) | data formatting | bytes 18874368 | tf_op jit(solution)/shard_map/reshape;squeeze;reshape | solution.py:27
  693.3 0.8 broadcast_in_dim.67
  694.1 30.2 %while.18 = (s32[]{:T(128)}, f32[128,4096]{1,0:T(8,128)}, bf16[1152,128]{1,0:T(8,128)(2,1)}, bf16[1152]{0:T(1024)(128)(2,1)S(1)}, bf16[1152,128]{1,0:T(8,128)(2,...) while((s32[]{:T(128)}, f32[128,4096]{1,0:T(8,128)}, ...), condition=%wide.region_6.7_spmd.clone, body=%wide.region_4.6_spmd.clone.sunk | while | flops 1224785920 | bytes 23371480 | solution.py:71
  694.1 4.8 fusion.32
  699.0 2.2 convolution_add_fusion.2
  701.1 1.7 fusion.33
  702.8 0.2 dynamic_update_slice.20
  703.1 4.8 fusion.32
  708.0 3.8 convolution_add_fusion.2
  711.8 1.7 fusion.33
  713.5 0.2 dynamic_update_slice.20
  713.7 4.8 fusion.32
  718.6 3.8 convolution_add_fusion.2
  722.4 1.7 fusion.33
  724.1 0.2 dynamic_update_slice.20
  724.3 0.8 all_to_all.25
  725.1 9.1 %all-to-all-start.4 = ((bf16[64,1,18]{2,1,0:T(2,128)(2,1)}), bf16[64,1,18]{2,1,0:T(2,128)(2,1)S(1)}, u32[]{:S(2)}, u32[]{:S(2)}) async-start(bf16[64,1,18]{2,1,0:T(2,128)(2,1)} %all_to_all.25), calls=%async_computation.4 | async-start | bytes 65536 | tf_op jit(solution)/shard_map/all_to_all | solution.py:116
  734.1 1.8 reshape_stack_reshape.4
  735.9 12.6 %all-to-all-done.4 = bf16[64,1,18]{2,1,0:T(2,128)(2,1)S(1)} async-done(((bf16[64,1,18]{2,1,0:T(2,128)(2,1)}), bf16[64,1,18]{2,1,0:T(2,128)(2,1)S(1)}, u32[]{:S(2)}, u32[]{:S(2)}) %all-to-all-start.4) | async-done | bytes 2336 | tf_op jit(solution)/shard_map/all_to_all | solution.py:116
  748.6 4.6 all-to-all-start.3
  753.4 0.1 reshape.144
  753.5 6.8 gather_fusion.4
  760.5 0.7 copy.24
  761.1 16.6 %all-to-all-done.3 = bf16[64,18,128]{2,1,0:T(8,128)(2,1)S(1)} async-done(((bf16[64,18,128]{2,1,0:T(8,128)(2,1)}), bf16[64,18,128]{2,1,0:T(8,128)(2,1)S(1)}, u32[]{:S(2)}, u32[]{:S(2)}) %all-to-all-start.3) | async-done | bytes 294944 | tf_op jit(solution)/shard_map/all_to_all | solution.py:115
  777.8 3.2 gather_fusion.3
  781.0 0.9 bitcast_select_fusion
  (47 shorter events, 1.8 us)
Async XLA Ops:
  7.2 56.2 %copy-start = (bf16[128,4096]{1,0:T(8,128)(2,1)S(1)}, bf16[128,4096]{1,0:T(8,128)(2,1)}, u32[]{:S(2)}) copy-start(bf16[128,4096]{1,0:T(8,128)(2,1)} %param.8) | copy-start | bytes 3145732
  7.2 52.1 %copy-start.2 = (bf16[128,8,128]{2,1,0:T(8,128)(2,1)S(1)}, bf16[128,8,128]{2,1,0:T(8,128)(2,1)}, u32[]{:S(2)}) copy-start(bf16[128,8,128]{2,1,0:T(8,128)(2,1)} %param.7) | copy-start | bytes 786436
  40.4 45.1 %all-to-all-start.1 = ((bf16[64,1,18]{2,1,0:T(2,128)(2,1)}), bf16[64,1,18]{2,1,0:T(2,128)(2,1)S(1)}, u32[]{:S(2)}, u32[]{:S(2)}) async-start(bf16[64,1,18]{2,1,0:T(2,128)(2,1)} %select_n.94), calls=%async_computation.1 | async-start | bytes 65536 | tf_op jit(solution)/shard_map/all_to_all | solution.py:111
  85.5 40.9 %all-to-all-start = ((bf16[64,18,128]{2,1,0:T(8,128)(2,1)}), bf16[64,18,128]{2,1,0:T(8,128)(2,1)S(1)}, u32[]{:S(2)}, u32[]{:S(2)}) async-start(bf16[64,18,128]{2,1,0:T(8,128)(2,1)} %broadcast_select_fusion.1), calls=%async_computation | async-start | bytes 786432 | tf_op jit(solution)/shard_map/all_to_all | solution.py:110
  126.4 552.8 %all-to-all-start.2 = ((bf16[64,18,4096]{2,1,0:T(8,128)(2,1)}), bf16[64,18,4096]{2,1,0:T(8,128)(2,1)}, u32[]{:S(2)}, u32[]{:S(2)}) async-start(bf16[64,18,4096]{2,1,0:T(8,128)(2,1)} %broadcast_select_fusion), calls=%async_computation.2 | async-start | bytes 25165824 | tf_op jit(solution)/shard_map/all_to_all | solution.py:109
  133.3 648.7 %reduce-scatter.2.cloned.1.call-start = ((), (), s32[]{:S(2)}) async-start(), calls=%async_computation.6 | async-start | bytes 2359296 | tf_op jit(solution)/shard_map/reduce_scatter | solution.py:124
  699.0 2.2 copy-start.3
  707.9 3.8 copy-start.3
  718.6 3.8 copy-start.3
  724.3 57.7 %copy-start.1 = (bf16[128,4096]{1,0:T(8,128)(2,1)S(1)}, bf16[128,4096]{1,0:T(8,128)(2,1)}, u32[]{:S(2)}) copy-start(bf16[128,4096]{1,0:T(8,128)(2,1)} %param.8) | copy-start | bytes 3145732
  725.1 23.5 %all-to-all-start.4 = ((bf16[64,1,18]{2,1,0:T(2,128)(2,1)}), bf16[64,1,18]{2,1,0:T(2,128)(2,1)S(1)}, u32[]{:S(2)}, u32[]{:S(2)}) async-start(bf16[64,1,18]{2,1,0:T(2,128)(2,1)} %all_to_all.25), calls=%async_computation.4 | async-start | bytes 65536 | tf_op jit(solution)/shard_map/all_to_all | solution.py:116
  748.6 29.2 %all-to-all-start.3 = ((bf16[64,18,128]{2,1,0:T(8,128)(2,1)}), bf16[64,18,128]{2,1,0:T(8,128)(2,1)S(1)}, u32[]{:S(2)}, u32[]{:S(2)}) async-start(bf16[64,18,128]{2,1,0:T(8,128)(2,1)} %reshape_stack_reshape.4), calls=%async_computation.3 | async-start | bytes 786432 | tf_op jit(solution)/shard_map/all_to_all | solution.py:115
Sparse Core Ops, SparseCore 0:
  724.4 33.3 reduce-scatter.1
where the time goes:
time: 790 us; the launch traced here: 789 us
  waiting for transfers between devices  590 us (75%)
  local copies, waits for them, and re-layouts  69.4 us (9%)
  starting transfers between devices  54.6 us (7%)
  other arithmetic  31.4 us (4%)
  matrix products  29.4 us (4%)
  between operations  14.3 us (2%)
    all_to_all x1, waiting for transfers between devices, local(): lax.all_to_all(send_grad, 'expert', split_axis=0, concat_axis=0, tiled=True)  545 us
    gather x2, local copies, waits for them, and re-layouts, local(): jnp.take(out_grad, source // top_count, axis=0, mode='fill', fill_value=0)  21.9 us
    all_to_all x1, starting transfers between devices, local(): lax.all_to_all(send_gate, 'expert', split_axis=0, concat_axis=0, tiled=True)  18.7 us
    another operation x3, other arithmetic  18.2 us
    all_to_all x1, waiting for transfers between devices, local(): lax.all_to_all(back_head, 'expert', split_axis=0, concat_axis=0, tiled=True)  16.6 us
  transfers between devices with their start and end apart: 6, of which 4 were waited for; matrix products, arithmetic and copies ran while one was open for 6% of the time, Pallas kernels for 0%

commit v1 on v0

v1 whole, which is shorter than its diff:
```python
import functools

import jax
import jax.numpy as jnp
from jax import lax
from jax.experimental import pallas as pl
from jax.experimental.pallas import tpu as pltpu
from jax.sharding import PartitionSpec as P

CAP = 1.5
F32 = jnp.float32
BF16 = jnp.bfloat16

SRC = 8
OWN = 8
TOK = 128
TOPK = 8
HD = 128
D = 4096
MAIN = 16
OVER = 2
ROWS = SRC * (MAIN + OVER)
META = D + TOPK * HD
WIDE = META + 128
STEP = 512


def iota(shape, axis):
    return lax.broadcasted_iota(jnp.int32, shape, axis).astype(F32)


def dispatch(base, x_ref, gx, gh, gg, hcat, qm, qo, po, over):
    upper = (iota((TOK, TOK), 0) < iota((TOK, TOK), 1)).astype(BF16)
    lane = iota((TOK, 128), 1)
    slot = iota((MAIN, TOK), 0)
    over[...] = jnp.zeros_like(over)

    def one_source(s, _):
        meta = x_ref[s, :, META:WIDE].astype(F32)
        routes = meta.T[TOPK : 2 * TOPK, :]
        named = [(routes == (base + 2 * j).astype(F32)).astype(F32) for j in range(OWN)]
        chosen = jnp.concatenate([jnp.sum(n, axis=0, keepdims=True) for n in named], axis=0)
        before = jnp.dot(chosen.astype(BF16), upper, preferred_element_type=F32)
        shift = (OVER * s - MAIN).astype(F32)
        columns = pl.ds(pl.multiple_of(s * TOK, TOK), TOK)
        picks = []
        for j in range(OWN):
            rows = slice(j * MAIN, (j + 1) * MAIN)
            pos = before[j : j + 1, :]
            spot = jnp.where(chosen[j : j + 1, :] > 0, pos, -1.0)
            picks.append((spot == slot).astype(F32))
            late = jnp.where(spot >= MAIN, spot + shift, -1.0)
            po[rows, columns] = (late == slot).astype(F32).astype(BF16)
            own = jnp.where(named[j] > 0, pos, -1.0)
            own_late = jnp.where(own >= MAIN, own + shift, -1.0)
            for k in range(TOPK):
                part = slice(k * TOK, (k + 1) * TOK)
                qm[rows, part] = (own[k : k + 1, :] == slot).astype(F32).astype(BF16)
                qo[rows, part] = (own_late[k : k + 1, :] == slot).astype(F32).astype(BF16)
        pick = jnp.concatenate(picks, axis=0).astype(BF16)
        for k in range(TOPK):
            part = slice(k * TOK, (k + 1) * TOK)
            hcat[part, 0:HD] = x_ref[s, :, D + k * HD : D + (k + 1) * HD]
            hcat[part, HD : 2 * HD] = jnp.where(lane == k, meta, 0.0).astype(BF16)
        out_rows = pl.ds(pl.multiple_of(s * MAIN, MAIN), MAIN)
        for c in range(0, D, STEP):
            block = jnp.dot(pick, x_ref[s, :, c : c + STEP], preferred_element_type=F32)
            gx[:, out_rows, c : c + STEP] = block.astype(BF16).reshape(OWN, MAIN, STEP)
        block = jnp.dot(qm[...], hcat[...], preferred_element_type=F32)
        gh[:, out_rows, :] = block[:, 0:HD].astype(BF16).reshape(OWN, MAIN, HD)
        gate = jnp.sum(block[:, HD:], axis=1, keepdims=True)
        gg[:, out_rows, :] = jnp.broadcast_to(gate, (OWN * MAIN, 128)).reshape(OWN, MAIN, 128)
        over[...] += jnp.dot(qo[...], hcat[...], preferred_element_type=F32)
        return 0

    lax.fori_loop(0, SRC, one_source, 0)
    tail = slice(SRC * MAIN, ROWS)
    width = 2 * 128
    for c in range(0, D, width):
        tokens = x_ref[:, :, c : c + width].reshape(SRC * TOK, width)
        block = jnp.dot(po[...], tokens, preferred_element_type=F32)
        gx[:, tail, c : c + width] = block.astype(BF16).reshape(OWN, SRC * OVER, width)
    gh[:, tail, :] = over[:, 0:HD].astype(BF16).reshape(OWN, SRC * OVER, HD)
    gate = jnp.sum(over[:, HD:], axis=1, keepdims=True)
    gg[:, tail, :] = jnp.broadcast_to(gate, (OWN * SRC * OVER, 128)).reshape(OWN, SRC * OVER, 128)


def owner_kernel(x_ref, w_ref, dw_ref, back_ref, gx, gh, gg, hcat, qm, qo, po, over):
    j = pl.program_id(0)
    me = lax.axis_index("dp")

    @pl.when(j == 0)
    def _():
        base = (me // 2) * 16 + lax.rem(me, 2)
        dispatch(base, x_ref, gx, gh, gg, hcat, qm, qo, po, over)

    heads = gh[j]
    gate = gg[j]
    head_grad = jnp.zeros((ROWS, HD), F32)
    gate_sum = jnp.zeros((ROWS, 128), F32)
    for c in range(0, D, STEP):
        weight = w_ref[:, 0, :, :, c : c + STEP].reshape(HD, STEP)
        pre = jnp.dot(heads, weight, preferred_element_type=F32)
        capped = jnp.tanh(pre * (1.0 / CAP))
        grad = gx[j, :, c : c + STEP].astype(F32)
        grad_capped = grad * capped
        rest = grad - grad_capped * capped
        parts = []
        for b in range(0, STEP, 128):
            gate_sum = gate_sum + grad_capped[:, b : b + 128]
            parts.append((gate * rest[:, b : b + 128]).astype(BF16))
        grad_pre = jnp.concatenate(parts, axis=1)
        head_grad = head_grad + lax.dot_general(
            grad_pre, weight, (((1,), (1,)), ((), ())), preferred_element_type=F32
        )
        grown = lax.dot_general(
            heads, grad_pre, (((0,), (0,)), ((), ())), preferred_element_type=F32
        )
        dw_ref[:, 0, :, :, c : c + STEP] = grown.astype(dw_ref.dtype).reshape(4, 2, 16, STEP)
    gate_grad = CAP * jnp.sum(gate_sum, axis=1, keepdims=True)
    back_ref[0, :, 0:HD] = head_grad.astype(BF16)
    back_ref[0, :, HD : 2 * HD] = jnp.broadcast_to(gate_grad, (ROWS, 128)).astype(BF16)


def owner_work(tokens, weights, sum_type):
    full = (4, 1, 2, 16, D)
    at_expert = lambda j: (0, j, 0, 0, 0)
    return pl.pallas_call(
        owner_kernel,
        grid=(OWN,),
        out_shape=(
            jax.ShapeDtypeStruct((4, OWN, 2, 16, D), sum_type),
            jax.ShapeDtypeStruct((OWN, ROWS, 2 * HD), BF16),
        ),
        in_specs=[
            pl.BlockSpec((SRC, TOK, WIDE), lambda j: (0, 0, 0), pipeline_mode=pl.Buffered(1)),
            pl.BlockSpec(full, at_expert),
        ],
        out_specs=(
            pl.BlockSpec(full, at_expert),
            pl.BlockSpec((1, ROWS, 2 * HD), lambda j: (j, 0, 0)),
        ),
        scratch_shapes=[
            pltpu.VMEM((OWN, ROWS, D), BF16),
            pltpu.VMEM((OWN, ROWS, HD), BF16),
            pltpu.VMEM((OWN, ROWS, 128), F32),
            pltpu.VMEM((TOPK * TOK, 2 * HD), BF16),
            pltpu.VMEM((OWN * MAIN, TOPK * TOK), BF16),
            pltpu.VMEM((OWN * MAIN, TOPK * TOK), BF16),
            pltpu.VMEM((OWN * MAIN, SRC * TOK), BF16),
            pltpu.VMEM((OWN * MAIN, 2 * HD), F32),
        ],
        compiler_params=pltpu.CompilerParams(vmem_limit_bytes=60 << 20),
    )(tokens, weights)


def return_kernel(routes_ref, back_ref, head_ref, gate_ref):
    routes = routes_ref[...]
    experts = lax.broadcasted_iota(jnp.int32, (TOK, 128), 1)
    named = [(routes[:, k : k + 1] == experts).astype(F32) for k in range(TOPK)]
    chosen = functools.reduce(lambda a, b: a + b, named)
    lower = (iota((TOK, TOK), 1) < iota((TOK, TOK), 0)).astype(BF16)
    before = jnp.dot(lower, chosen.astype(BF16), preferred_element_type=F32)
    rows = lax.broadcasted_iota(jnp.int32, (TOK, SRC * ROWS), 1)
    gates = jnp.zeros((TOK, 128), F32)
    for k in range(TOPK):
        expert = routes[:, k : k + 1]
        slot = jnp.sum(named[k] * before, axis=1, keepdims=True).astype(jnp.int32)
        owner = 2 * (expert >> 4) + (expert & 1)
        index = (expert & 15) >> 1
        place = jnp.where(
            slot < MAIN, index * MAIN + slot, OWN * MAIN + OVER * index + slot - MAIN
        )
        pick = (rows == owner * ROWS + place).astype(F32).astype(BF16)
        block = jnp.dot(pick, back_ref[...], preferred_element_type=F32)
        head_ref[:, k * HD : (k + 1) * HD] = block[:, 0:HD].astype(BF16)
        gates = jnp.where(experts == k, block[:, HD:], gates)
    gate_ref[...] = gates[:, 0:TOPK].astype(BF16)


def put_back(routes, back):
    return pl.pallas_call(
        return_kernel,
        out_shape=(
            jax.ShapeDtypeStruct((TOK, TOPK * HD), BF16),
            jax.ShapeDtypeStruct((TOK, TOPK), BF16),
        ),
        compiler_params=pltpu.CompilerParams(vmem_limit_bytes=32 << 20),
    )(routes, back)


def swap_pairs(mesh):
    pairs = []
    for dp in range(mesh.shape["dp"]):
        for expert in range(mesh.shape["expert"]):
            x, core = divmod(dp, 2)
            y, z = divmod(expert, 16)
            to_dp = 2 * y + z % 2
            to_expert = 16 * x + z - z % 2 + core
            pairs.append((dp * 64 + expert, to_dp * 64 + to_expert))
    return pairs


def local(head_outputs, out_grad, gate_weights, route_ids, out_proj, pairs, sum_type=F32):
    axes = ("dp", "expert")
    me = lax.axis_index("dp")
    part = lax.dynamic_slice_in_dim(out_proj[0], me * 16, 16, 0)
    part = lax.ppermute(part, axes, pairs)
    weights = lax.all_gather(part, "expert")
    packed = jnp.concatenate(
        [
            out_grad,
            head_outputs.reshape(TOK, TOPK * HD),
            gate_weights,
            route_ids.astype(BF16),
            jnp.zeros((TOK, 128 - 2 * TOPK), BF16),
        ],
        axis=1,
    )
    tokens = lax.all_gather(packed, "dp")
    sums, back = owner_work(tokens, weights.reshape(4, OWN, 2, 16, D), sum_type)
    grad_proj = lax.psum_scatter(
        sums.reshape(64, 16, D), "expert", scatter_dimension=0, tiled=False
    )
    grad_proj = lax.ppermute(grad_proj.astype(F32), axes, pairs)
    main = back[:, : SRC * MAIN].reshape(OWN, SRC, MAIN, 2 * HD).transpose(1, 0, 2, 3)
    late = back[:, SRC * MAIN :].reshape(OWN, SRC, OVER, 2 * HD).transpose(1, 0, 2, 3)
    send = jnp.concatenate(
        [main.reshape(SRC, OWN * MAIN, 2 * HD), late.reshape(SRC, OWN * OVER, 2 * HD)], axis=1
    )
    got = lax.all_to_all(send, "dp", split_axis=0, concat_axis=0, tiled=True)
    grad_head, grad_gate = put_back(route_ids, got.reshape(SRC * ROWS, 2 * HD))
    return grad_head.reshape(TOK, TOPK, HD), grad_gate, grad_proj[None]


def solution(mesh):
    return jax.shard_map(
        functools.partial(local, pairs=swap_pairs(mesh)),
        mesh=mesh,
        in_specs=(
            P(("dp", "expert"), None, None),
            P(("dp", "expert"), None),
            P(("dp", "expert"), None),
            P(("dp", "expert"), None),
            P("expert", None, None),
        ),
        out_specs=(
            P(("dp", "expert"), None, None),
            P(("dp", "expert"), None),
            P("expert", "dp", None),
        ),
        check_vma=False,
    )
```

time: 790 us -> 1030 us (1.30)
  waiting for transfers between devices: 590 us -> 960 us
  local copies, waits for them, and re-layouts: 69.4 us -> 9.21 us
  starting transfers between devices: 54.6 us -> 14.5 us
  Pallas kernels: 0 us -> 32.1 us
  other arithmetic: 31.4 us -> 1.57 us
  matrix products: 29.4 us -> 0 us
    reduce_scatter x1, waiting for transfers between devices: 0.01 us -> 724 us  [local(): lax.psum_scatter(sums.reshape(64, 16, D), 'expert', scatter_dimension=0,...]
    all_to_all x5 -> x1, waiting for transfers between devices: 590 us -> 0.01 us  [local(): got = lax.all_to_all(send, 'dp', split_axis=0, concat_axis=0, tiled=True)]
    all_gather x0 -> x2, waiting for transfers between devices: none -> 216 us  [the longest x1 153 us: local(): weights = lax.all_gather(part, 'expert')]
    all_to_all x5 -> x1, starting transfers between devices: 54.4 us -> 5.83 us  [local(): got = lax.all_to_all(send, 'dp', split_axis=0, concat_axis=0, tiled=True)]
    gather x8 -> x0, local copies, waits for them, and re-layouts: 42.3 us -> none  [the longest x2 21.9 us: local(): jnp.take(out_grad, source // top_count, axis=0, mode='fill', fill_value=0)]
    pallas_call x0 -> x2, Pallas kernels: none -> 32.1 us  [the longest x1 30.5 us: owner_work(): pl.pallas_call(owner_kernel, grid=(OWN,), out_shape=(jax.ShapeDtypeStruct...]
    dot_general x9 -> x0, matrix products: 29.4 us -> none  [the longest x3 14.5 us: advance(): pre_cap = jnp.dot(head_block, weight, preferred_element_type=jnp.float32)]
    ppermute x0 -> x2, waiting for transfers between devices: none -> 19.8 us  [the longest x1 10.2 us: local(): grad_proj = lax.ppermute(grad_proj.astype(F32), axes, pairs)]
  transfers between devices with their start and end apart: 6 -> 6, of which waited for: 4 -> 5; matrix products, arithmetic and copies ran while one was open for 6% -> 1% of each run, Pallas kernels for 0% -> 0%
where the time goes in v1:
time: 1030 us
  waiting for transfers between devices  960 us (93%)
  Pallas kernels  32.1 us (3%)
  starting transfers between devices  14.5 us (1%)
  between operations  13.9 us (1%)
    reduce_scatter x1, waiting for transfers between devices, local(): lax.psum_scatter(sums.reshape(64, 16, D), 'expert', scatter_dimension=0,...  724 us
    all_gather x1, waiting for transfers between devices, local(): weights = lax.all_gather(part, 'expert')  153 us
    all_gather x1, waiting for transfers between devices, local(): tokens = lax.all_gather(packed, 'dp')  62.5 us
    pallas_call x1, Pallas kernels, owner_work(): pl.pallas_call(owner_kernel, grid=(OWN,), out_shape=(jax.ShapeDtypeStruct...  30.5 us
  transfers between devices with their start and end apart: 6, of which 5 were waited for; matrix products, arithmetic and copies ran while one was open for 1% of the time, Pallas kernels for 0%

profile of v1, /device:TPU:6, one launch (start us, length us, event | category | flops | bytes accessed | tf_op | source)
XLA Modules:
  0.0 1031.3 jit_solution(3595849816631350713)
XLA Ops:
  7.2 0.0 copy-start
  7.2 0.0 copy-start.1
  7.2 0.0 all-gather.7.cloned.1.call-start
  7.2 1.2 copy-done
  8.4 4.8 collective-permute-start
  13.3 9.5 collective-permute-done
  22.8 0.0 copy-start.3
  22.8 0.7 copy-done.3
  23.5 0.0 all-gather.7.cloned.1.call-update
  23.5 0.0 all-gather.5.cloned.1.call-start
  23.5 1.0 copy.17
  24.5 0.7 convert_element_type.3
  25.2 0.1 copy.9
  25.4 0.8 copy.8
  26.2 0.0 copy-done.1
  26.2 2.0 concatenate.6
  28.2 0.0 all-gather.5.cloned.1.call-update
  28.2 0.0 reduce-scatter.2.cloned.1.call-start
  28.2 153.3 %all-gather.7.cloned.1.call-done = bf16[1024,4096]{1,0:T(8,128)(2,1)} async-done(((bf16[16,4096]{1,0:T(8,128)(2,1)}), bf16[1024,4096]{1,0:T(8,128)(2,1)}) %all-gather.7.cloned.1.call-update) | async-done | bytes 8388624 | tf_op jit(solution)/shard_map/all_gather | solution.py:209
  181.5 62.5 %all-gather.5.cloned.1.call-done = bf16[1024,5248]{1,0:T(8,128)(2,1)} async-done(((bf16[128,5248]{1,0:T(8,128)(2,1)}), bf16[1024,5248]{1,0:T(8,128)(2,1)}) %all-gather.5.cloned.1.call-update) | async-done | bytes 10747920 | tf_op jit(solution)/shard_map/all_gather | solution.py:220
  244.1 30.5 %shard_map.76 = (f32[4,8,2,16,4096]{4,3,2,1,0:T(8,128)}, bf16[8,144,256]{2,1,0:T(8,128)(2,1)}) custom-call(bf16[8,128,5248]{2,1,0:T(8,128)(2,1)} %bitcast.22, bf16[4,8,2,16,4096]{4,3,2,1,0:T(8,128)(2,1)} %bitcast.23), custom_call_target="tpu_custom_call" | custom-call | tf_op jit(solution)/shard_map/pallas_call | solution.py:128
  274.5 0.0 copy-start.2
  274.5 0.0 reduce-scatter.2.cloned.1.call-update
  274.5 1.0 copy-done.2
  275.7 0.0 copy-start.4
  275.8 0.9 pad_maximum_fusion
  276.7 5.8 all-to-all-start
  282.5 724.5 %reduce-scatter.2.cloned.1.call-done = f32[1,16,4096]{2,1,0:T(8,128)} async-done(((f32[64,16,4096]{2,1,0:T(8,128)}), f32[1,16,4096]{2,1,0:T(8,128)}) %reduce-scatter.2.cloned.1.call-update) | async-done | bytes 262160 | tf_op jit(solution)/shard_map/reduce_scatter | solution.py:222
  1007.0 3.7 collective-permute-start.1
  1010.7 0.0 copy-done.4
  1010.7 0.1 copy.12.routes_ref
  1010.8 0.0 all-to-all-done
  1010.8 1.6 shard_map.77
  1012.4 0.8 copy.15
  1013.2 0.7 copy.13
  1013.8 10.2 collective-permute-done.1
  1024.1 0.7 copy.19
  (8 shorter events, 0.2 us)
Async XLA Ops:
  7.2 1.2 copy-start
  7.2 19.0 %copy-start.1 = (bf16[128,4096]{1,0:T(8,128)(2,1)S(1)}, bf16[128,4096]{1,0:T(8,128)(2,1)}, u32[]{:S(2)}) copy-start(bf16[128,4096]{1,0:T(8,128)(2,1)} %param.6) | copy-start | bytes 3145732
  7.2 174.4 %all-gather.7.cloned.1.call-start = ((), (), s32[]{:S(2)}) async-start(), calls=%async_computation.4 | async-start | bytes 8519680 | tf_op jit(solution)/shard_map/all_gather | solution.py:209
  8.4 14.4 %collective-permute-start = (bf16[16,4096]{1,0:T(8,128)(2,1)S(1)}, bf16[16,4096]{1,0:T(8,128)(2,1)S(1)}, u32[]{:S(2)}, u32[]{:S(2)}) collective-permute-start(bf16[16,4096]{1,0:T(8,128)(2,1)S(1)} %dynamic-slice_bitcast_fusion), channel_id=1, source_target_pairs={{0,0},{1,64},{2,2},{3,66},{4,4},{5,68},{6,6},{7,70},{8,8},{9,72},{... | collective-permute-start | bytes 393224 | tf_op jit(solution)/shard_map/ppermute | solution.py:208
  22.8 0.7 copy-start.3
  23.5 220.6 %all-gather.5.cloned.1.call-start = ((), (), s32[]{:S(2)}) async-start(), calls=%async_computation.3 | async-start | bytes 12091392 | tf_op jit(solution)/shard_map/all_gather | solution.py:220
  28.2 978.8 %reduce-scatter.2.cloned.1.call-start = ((), (), s32[]{:S(2)}) async-start(), calls=%async_computation.2 | async-start | bytes 17039360 | tf_op jit(solution)/shard_map/reduce_scatter | solution.py:222
  274.5 1.1 copy-start.2
  275.7 735.0 %copy-start.4 = (s32[128,8]{0,1:T(8,128)S(1)}, s32[128,8]{0,1:T(8,128)}, u32[]{:S(2)}) copy-start(s32[128,8]{0,1:T(8,128)} %param.8) | copy-start | bytes 12292
  276.7 734.1 %all-to-all-start = ((bf16[8,144,256]{2,1,0:T(8,128)(2,1)}), bf16[8,144,256]{2,1,0:T(8,128)(2,1)S(1)}, u32[]{:S(2)}, u32[]{:S(2)}) async-start(bf16[8,144,256]{2,1,0:T(8,128)(2,1)} %pad_maximum_fusion), calls=%async_computation | async-start | bytes 1179648 | tf_op jit(solution)/shard_map/all_to_all | solution.py:231
  1007.0 17.1 %collective-permute-start.1 = (f32[16,4096]{1,0:T(8,128)}, f32[16,4096]{1,0:T(8,128)S(1)}, u32[]{:S(2)}, u32[]{:S(2)}) collective-permute-start(f32[16,4096]{1,0:T(8,128)} %bitcast.31), channel_id=1, source_target_pairs={{0,0},{1,64},{2,2},{3,66},{4,4},{5,68},{6,6},{7,70},{8,8},{9,72},{... | collective-permute-start | bytes 786440 | tf_op jit(solution)/shard_map/ppermute | solution.py:225
Sparse Core Ops, SparseCore 0:
  23.6 157.8 all-gather.6
  183.7 60.3 all-gather.4
  274.7 732.2 reduce-scatter.1

commit v2 on v1

--- a/solution.py
+++ b/solution.py
@@ -29,13 +29,14 @@
     return lax.broadcasted_iota(jnp.int32, shape, axis).astype(F32)
 
 
-def dispatch(base, x_ref, gx, gh, gg, hcat, qm, qo, po, over):
+def dispatch(base, x_ref, gx, gh, gg, hcat, qm, qo, po, over, arrived):
     upper = (iota((TOK, TOK), 0) < iota((TOK, TOK), 1)).astype(BF16)
     lane = iota((TOK, 128), 1)
     slot = iota((MAIN, TOK), 0)
     over[...] = jnp.zeros_like(over)
 
     def one_source(s, _):
+        arrived(s)
         meta = x_ref[s, :, META:WIDE].astype(F32)
         routes = meta.T[TOPK : 2 * TOPK, :]
         named = [(routes == (base + 2 * j).astype(F32)).astype(F32) for j in range(OWN)]
@@ -85,21 +86,151 @@
     gg[:, tail, :] = jnp.broadcast_to(gate, (OWN * SRC * OVER, 128)).reshape(OWN, SRC * OVER, 128)
 
 
-def owner_kernel(x_ref, w_ref, dw_ref, back_ref, gx, gh, gg, hcat, qm, qo, po, over):
-    j = pl.program_id(0)
-    me = lax.axis_index("dp")
-
-    @pl.when(j == 0)
+MESH = pl.DeviceIdType.MESH
+HALF = D // 2
+FAR = 8
+
+
+def place():
+    dp, expert = lax.axis_index("dp"), lax.axis_index("expert")
+    y, z = expert // 16, lax.rem(expert, 16)
+    x, core = dp // 2, lax.rem(dp, 2)
+    odd = lax.rem(z, 2)
+    partner = (2 * y + odd, 16 * x + z - odd + core)
+    alone = jnp.logical_and(x == y, core == odd)
+    return dp, y, z, partner, alone
+
+
+def meet(peers, partner, alone):
+    barrier = pltpu.get_barrier_semaphore()
+    for peer in peers:
+        pl.semaphore_signal(barrier, inc=1, device_id=peer, device_id_type=MESH)
+
+    @pl.when(jnp.logical_not(alone))
     def _():
-        base = (me // 2) * 16 + lax.rem(me, 2)
-        dispatch(base, x_ref, gx, gh, gg, hcat, qm, qo, po, over)
-
+        pl.semaphore_signal(barrier, inc=1, device_id=partner, device_id_type=MESH)
+
+    pl.semaphore_wait(barrier, len(peers) + jnp.where(alone, 0, 1))
+
+
+def send(src, dst, send_sem, recv_sem, device):
+    return pltpu.make_async_remote_copy(
+        src_ref=src,
+        dst_ref=dst,
+        send_sem=send_sem,
+        recv_sem=recv_sem,
+        device_id=device,
+        device_id_type=MESH,
+    )
+
+
+def gather_kernel(proj_ref, w_ref, own, own_sem, keep_sem, zs, zr, ys, yr, fs, fr):
+    dp, y, z, partner, alone = place()
+    at = lambda row, col: (dp, row * 16 + col)
+    ring = lambda v, step, n: lax.rem(v + step + n, n)
+    up, down = at(ring(y, 1, 4), z), at(ring(y, -1, 4), z)
+    right, left = at(y, ring(z, 1, 16)), at(y, ring(z, -1, 16))
+    meet((up, down, right, left), partner, alone)
+
+    mine = proj_ref.at[pl.ds(pl.multiple_of(dp * 16, 16), 16), :]
+    trade = send(mine, own, own_sem.at[0], own_sem.at[1], partner)
+    local = pltpu.make_async_copy(mine, own, own_sem.at[1])
+
+    @pl.when(alone)
+    def _():
+        local.start()
+        local.wait()
+
+    @pl.when(jnp.logical_not(alone))
+    def _():
+        trade.start()
+        trade.wait()
+
+    keep = pltpu.make_async_copy(own, w_ref.at[y, z], keep_sem)
+    keep.start()
+
+    def along_z(src, col, way, hop):
+        return send(src, w_ref.at[y, col], zs.at[way, hop], zr.at[way, hop], (right, left)[way])
+
+    def along_y(src, col, way):
+        return send(src, w_ref.at[y, col], ys.at[way, col], yr.at[way, col], (up, down)[way])
+
+    def spread(src, col):
+        along_y(src, col, 0).start()
+        along_y(src, col, 1).start()
+
+    along_z(own, z, 0, 0).start()
+    along_z(own, z, 1, 0).start()
+    spread(own, z)
+    for hop in range(1, FAR + 1):
+        for way in range(2 if hop < FAR else 1):
+            col = ring(z, -hop if way == 0 else hop, 16)
+            block = w_ref.at[y, col]
+            along_z(block, col, way, hop - 1).wait_recv()
+            if hop < FAR - way:
+                along_z(block, col, way, hop).start()
+            spread(block, col)
+
+    def forward(row, col, way):
+        half = pl.ds(way * HALF, HALF)
+        block = w_ref.at[row, col, :, half]
+        return send(block, block, fs.at[way, col], fr.at[way, col], (up, down)[way])
+
+    below, above, across = ring(y, -1, 4), ring(y, 1, 4), ring(y, 2, 4)
+    order = [0]
+    for hop in range(1, FAR + 1):
+        order += [-hop, hop] if hop < FAR else [-hop]
+    for step in order:
+        col = ring(z, step, 16)
+        send(own, w_ref.at[below, col], ys.at[0, col], yr.at[0, col], up).wait_recv()
+        forward(below, col, 0).start()
+        send(own, w_ref.at[above, col], ys.at[1, col], yr.at[1, col], down).wait_recv()
+        forward(above, col, 1).start()
+    for step in order:
+        col = ring(z, step, 16)
+        forward(across, col, 0).wait_recv()
+        forward(across, col, 1).wait_recv()
+    keep.wait()
+    for hop in range(FAR):
+        for way in range(2):
+            if hop < FAR - way:
+                along_z(own, z, way, hop).wait_send()
+    for col in range(16):
+        for way in range(2):
+            along_y(own, col, way).wait_send()
+            forward(across, col, way).wait_send()
+
+
+def gather_weights(proj):
+    sems = pltpu.SemaphoreType.DMA
+    return pl.pallas_call(
+        gather_kernel,
+        out_shape=jax.ShapeDtypeStruct((4, 16, 16, D), BF16),
+        in_specs=[pl.BlockSpec(memory_space=pl.ANY)],
+        out_specs=pl.BlockSpec(memory_space=pl.ANY),
+        scratch_shapes=[
+            pltpu.VMEM((16, D), BF16),
+            sems((2,)),
+            sems,
+            sems((2, FAR)),
+            sems((2, FAR)),
+            sems((2, 16)),
+            sems((2, 16)),
+            sems((2, 16)),
+            sems((2, 16)),
+        ],
+        compiler_params=pltpu.CompilerParams(collective_id=0, has_side_effects=True),
+        cost_estimate=pl.CostEstimate(flops=0, bytes_accessed=1 << 28, transcendentals=0),
+    )(proj)
+
+
+def expert_step(i, j, wbuf, slot, gx, gh, gg, part, ret, late):
     heads = gh[j]
     gate = gg[j]
     head_grad = jnp.zeros((ROWS, HD), F32)
     gate_sum = jnp.zeros((ROWS, 128), F32)
     for c in range(0, D, STEP):
-        weight = w_ref[:, 0, :, :, c : c + STEP].reshape(HD, STEP)
+        weight = wbuf[slot, :, :, :, c : c + STEP].reshape(HD, STEP)
         pre = jnp.dot(heads, weight, preferred_element_type=F32)
         capped = jnp.tanh(pre * (1.0 / CAP))
         grad = gx[j, :, c : c + STEP].astype(F32)
@@ -116,41 +247,229 @@
         grown = lax.dot_general(
             heads, grad_pre, (((0,), (0,)), ((), ())), preferred_element_type=F32
         )
-        dw_ref[:, 0, :, :, c : c + STEP] = grown.astype(dw_ref.dtype).reshape(4, 2, 16, STEP)
+        part[i, :, :, c : c + STEP] = grown.astype(BF16).reshape(4, 32, STEP)
     gate_grad = CAP * jnp.sum(gate_sum, axis=1, keepdims=True)
-    back_ref[0, :, 0:HD] = head_grad.astype(BF16)
-    back_ref[0, :, HD : 2 * HD] = jnp.broadcast_to(gate_grad, (ROWS, 128)).astype(BF16)
-
-
-def owner_work(tokens, weights, sum_type):
-    full = (4, 1, 2, 16, D)
-    at_expert = lambda j: (0, j, 0, 0, 0)
+    both = jnp.concatenate([head_grad, jnp.broadcast_to(gate_grad, (ROWS, 128))], axis=1)
+    both = both.astype(BF16)
+    rows = pl.ds(pl.multiple_of(j * MAIN, MAIN), MAIN)
+    ret[:, rows, :] = both[0 : SRC * MAIN].reshape(SRC, MAIN, 2 * HD)
+    late[rows, :] = both[SRC * MAIN :]
+
+
+def owner_kernel(
+    x_ref, w_ref, out_ref, got_ref,
+    xbuf, wbuf, gx, gh, gg, hcat, qm, qo, po, over, part, a_in, b_in, comb, zl, zr, zout, ret, late,
+    x_sem, w_sem, ps, pr, cs, cr, zs, zlr, zrr, out_sem, rs, rr, keep_sem,
+):
+    dp, y, z, partner, alone = place()
+    ring = lambda v, step, n: lax.rem(v + step + n, n)
+    yu, yd, y2 = ring(y, 1, 4), ring(y, -1, 4), ring(y, 2, 4)
+    up, down = (dp, yu * 16 + z), (dp, yd * 16 + z)
+    right, left = (dp, y * 16 + ring(z, 1, 16)), (dp, y * 16 + ring(z, -1, 16))
+    here = y * 16 + z
+    others = [(lax.rem(dp + k, SRC), here) for k in range(1, SRC)]
+    base = (dp // 2) * 16 + lax.rem(dp, 2)
+
+    def expert_at(i):
+        away = 4 - (i + 1) // 2
+        return lax.rem(z // 2 + OWN + jnp.where(lax.rem(i, 2) == 1, away, -away), OWN)
+
+    def token_copy(s):
+        return pltpu.make_async_copy(x_ref.at[s], xbuf.at[s], x_sem.at[s])
+
+    def weight_copy(i):
+        slot = lax.rem(i, 2)
+        return pltpu.make_async_copy(w_ref.at[:, expert_at(i)], wbuf.at[slot], w_sem.at[slot])
+
+    for s in range(SRC):
+        token_copy(s).start()
+    weight_copy(0).start()
+    meet([up, down, right, left] + others, partner, alone)
+    dispatch(base, xbuf, gx, gh, gg, hcat, qm, qo, po, over, lambda s: token_copy(s).wait())
+
+    low, high = pl.ds(0, HALF), pl.ds(HALF, HALF)
+
+    def first_sends(i):
+        return (
+            send(part.at[i, y2, :, low], a_in.at[i, 0], ps.at[i, 0], pr.at[i, 0], up),
+            send(part.at[i, y2, :, high], a_in.at[i, 1], ps.at[i, 1], pr.at[i, 1], down),
+            send(part.at[i, yu, :, high], b_in.at[i, 0, :, high], ps.at[i, 2], pr.at[i, 2], up),
+            send(part.at[i, yd, :, low], b_in.at[i, 1, :, low], ps.at[i, 3], pr.at[i, 3], down),
+        )
+
+    def second_sends(i):
+        return (
+            send(comb.at[i, 0], b_in.at[i, 0, :, low], cs.at[i, 0], cr.at[i, 0], up),
+            send(comb.at[i, 1], b_in.at[i, 1, :, high], cs.at[i, 1], cr.at[i, 1], down),
+        )
+
+    def combine(i):
+        first, second = first_sends(i), second_sends(i)
+        first[0].wait_recv()
+        comb[i, 0] = (part[i, yu, :, low].astype(F32) + a_in[i, 0].astype(F32)).astype(BF16)
+        second[0].start()
+        first[1].wait_recv()
+        comb[i, 1] = (part[i, yd, :, high].astype(F32) + a_in[i, 1].astype(F32)).astype(BF16)
+        second[1].start()
+
+    def to_right(k, slot):
+        return send(zout.at[k], zl.at[slot], zs.at[k], zlr.at[slot], right)
+
+    def to_left(k, slot):
+        return send(zout.at[k], zr.at[slot], zs.at[k], zrr.at[slot], left)
+
+    def to_partner(k):
+        return send(zout.at[k], out_ref, zs.at[k], out_sem, partner)
+
+    def finish(i):
+        for one in first_sends(i)[2:] + second_sends(i):
+            one.wait_recv()
+        total = (
+            part[i, y].astype(F32) + b_in[i, 0].astype(F32) + b_in[i, 1].astype(F32)
+        )
+        j = expert_at(i)
+        for c in range(2):
+            k = 2 * i + c
+            zout[k] = total[16 * c : 16 * (c + 1)]
+            ahead = lax.rem(2 * j + c - z + 16, 16)
+            behind = lax.rem(16 - ahead, 16)
+
+            @pl.when(ahead < FAR)
+            def _():
+                to_right(k, ahead).wait_recv()
+                zout[k] += zl[ahead]
+
+            @pl.when(behind < FAR - 1)
+            def _():
+                to_left(k, behind).wait_recv()
+                zout[k] += zr[behind]
+
+            @pl.when(jnp.logical_and(ahead >= 1, ahead <= FAR))
+            def _():
+                to_right(k, ahead - 1).start()
+
+            @pl.when(ahead > FAR)
+            def _():
+                to_left(k, behind - 1).start()
+
+            @pl.when(jnp.logical_and(ahead == 0, alone))
+            def _():
+                pltpu.make_async_copy(zout.at[k], out_ref, zs.at[k]).start()
+
+            @pl.when(jnp.logical_and(ahead == 0, jnp.logical_not(alone)))
+            def _():
+                to_partner(k).start()
+
+    def returns():
+        out = []
+        for k in range(1, SRC):
+            to = lax.rem(dp + k, SRC)
+            out.append(send(ret.at[to], got_ref.at[dp], rs.at[k], rr.at[k], others[k - 1]))
+        return out
+
+    keep = pltpu.make_async_copy(ret.at[dp], got_ref.at[dp], keep_sem)
+
+    def one_expert(i, _):
+        @pl.when(i < OWN)
+        def _():
+            @pl.when(i + 1 < OWN)
+            def _():
+                weight_copy(i + 1).start()
+
+            weight_copy(i).wait()
+            expert_step(i, expert_at(i), wbuf, lax.rem(i, 2), gx, gh, gg, part, ret, late)
+            for one in first_sends(i):
+                one.start()
+
+        @pl.when(i == OWN - 1)
+        def _():
+            to = lax.broadcasted_iota(jnp.int32, (OWN * MAIN, OWN * MAIN), 0)
+            source = lax.broadcasted_iota(jnp.int32, (OWN * MAIN, OWN * MAIN), 1)
+            want = (lax.rem(to, 16) // 2) * 16 + (to // 16) * 2 + lax.rem(to, 2)
+            shuffle = (source == want).astype(F32).astype(BF16)
+            moved = jnp.dot(shuffle, late[...], preferred_element_type=F32).astype(BF16)
+            ret[:, OWN * MAIN :, :] = moved.reshape(SRC, OWN * OVER, 2 * HD)
+            for one in returns():
+                one.start()
+            keep.start()
+
+        @pl.when(jnp.logical_and(i >= 1, i <= OWN))
+        def _():
+            combine(i - 1)
+
+        @pl.when(i >= 2)
+        def _():
+            finish(i - 2)
+
+        return 0
+
+    lax.fori_loop(0, OWN + 2, one_expert, 0)
+    for one in returns():
+        one.wait()
+    keep.wait()
+
+    @pl.when(jnp.logical_not(alone))
+    def _():
+        to_partner(0).wait_recv()
+
+    def drain(i, _):
+        for one in first_sends(i) + second_sends(i):
+            one.wait_send()
+        to_right(2 * i, 0).wait_send()
+        to_right(2 * i + 1, 0).wait_send()
+        return 0
+
+    lax.fori_loop(0, OWN, drain, 0)
+
+
+def owner_work(tokens, weights):
+    sems = pltpu.SemaphoreType.DMA
+    vmem = pltpu.VMEM
     return pl.pallas_call(
         owner_kernel,
-        grid=(OWN,),
         out_shape=(
-            jax.ShapeDtypeStruct((4, OWN, 2, 16, D), sum_type),
-            jax.ShapeDtypeStruct((OWN, ROWS, 2 * HD), BF16),
+            jax.ShapeDtypeStruct((16, D), F32),
+            jax.ShapeDtypeStruct((SRC, ROWS, 2 * HD), BF16),
         ),
-        in_specs=[
-            pl.BlockSpec((SRC, TOK, WIDE), lambda j: (0, 0, 0), pipeline_mode=pl.Buffered(1)),
-            pl.BlockSpec(full, at_expert),
+        in_specs=[pl.BlockSpec(memory_space=pl.ANY)] * 2,
+        out_specs=(pl.BlockSpec(memory_space=pl.ANY),) * 2,
+        scratch_shapes=[
+            vmem((SRC, TOK, WIDE), BF16),
+            vmem((2, 4, 2, 16, D), BF16),
+            vmem((OWN, ROWS, D), BF16),
+            vmem((OWN, ROWS, HD), BF16),
+            vmem((OWN, ROWS, 128), F32),
+            vmem((TOPK * TOK, 2 * HD), BF16),
+            vmem((OWN * MAIN, TOPK * TOK), BF16),
+            vmem((OWN * MAIN, TOPK * TOK), BF16),
+            vmem((OWN * MAIN, SRC * TOK), BF16),
+            vmem((OWN * MAIN, 2 * HD), F32),
+            vmem((OWN, 4, 32, D), BF16),
+            vmem((OWN, 2, 32, HALF), BF16),
+            vmem((OWN, 2, 32, D), BF16),
+            vmem((OWN, 2, 32, HALF), BF16),
+            vmem((FAR, 16, D), F32),
+            vmem((FAR - 1, 16, D), F32),
+            vmem((2 * OWN, 16, D), F32),
+            vmem((SRC, ROWS, 2 * HD), BF16),
+            vmem((OWN * MAIN, 2 * HD), BF16),
+            sems((SRC,)),
+            sems((2,)),
+            sems((OWN, 4)),
+            sems((OWN, 4)),
+            sems((OWN, 2)),
+            sems((OWN, 2)),
+            sems((2 * OWN,)),
+            sems((FAR,)),
+            sems((FAR - 1,)),
+            sems,
+            sems((SRC,)),
+            sems((SRC,)),
+            sems,
         ],
-        out_specs=(
-            pl.BlockSpec(full, at_expert),
-            pl.BlockSpec((1, ROWS, 2 * HD), lambda j: (j, 0, 0)),
+        compiler_params=pltpu.CompilerParams(
+            collective_id=1, has_side_effects=True, vmem_limit_bytes=67043328
         ),
-        scratch_shapes=[
-            pltpu.VMEM((OWN, ROWS, D), BF16),
-            pltpu.VMEM((OWN, ROWS, HD), BF16),
-            pltpu.VMEM((OWN, ROWS, 128), F32),
-            pltpu.VMEM((TOPK * TOK, 2 * HD), BF16),
-            pltpu.VMEM((OWN * MAIN, TOPK * TOK), BF16),
-            pltpu.VMEM((OWN * MAIN, TOPK * TOK), BF16),
-            pltpu.VMEM((OWN * MAIN, SRC * TOK), BF16),
-            pltpu.VMEM((OWN * MAIN, 2 * HD), F32),
-        ],
-        compiler_params=pltpu.CompilerParams(vmem_limit_bytes=60 << 20),
     )(tokens, weights)
 
 
@@ -189,24 +508,7 @@
     )(routes, back)
 
 
-def swap_pairs(mesh):
-    pairs = []
-    for dp in range(mesh.shape["dp"]):
-        for expert in range(mesh.shape["expert"]):
-            x, core = divmod(dp, 2)
-            y, z = divmod(expert, 16)
-            to_dp = 2 * y + z % 2
-            to_expert = 16 * x + z - z % 2 + core
-            pairs.append((dp * 64 + expert, to_dp * 64 + to_expert))
-    return pairs
-
-
-def local(head_outputs, out_grad, gate_weights, route_ids, out_proj, pairs, sum_type=F32):
-    axes = ("dp", "expert")
-    me = lax.axis_index("dp")
-    part = lax.dynamic_slice_in_dim(out_proj[0], me * 16, 16, 0)
-    part = lax.ppermute(part, axes, pairs)
-    weights = lax.all_gather(part, "expert")
+def local(head_outputs, out_grad, gate_weights, route_ids, out_proj):
     packed = jnp.concatenate(
         [
             out_grad,
@@ -218,24 +520,15 @@
         axis=1,
     )
     tokens = lax.all_gather(packed, "dp")
-    sums, back = owner_work(tokens, weights.reshape(4, OWN, 2, 16, D), sum_type)
-    grad_proj = lax.psum_scatter(
-        sums.reshape(64, 16, D), "expert", scatter_dimension=0, tiled=False
-    )
-    grad_proj = lax.ppermute(grad_proj.astype(F32), axes, pairs)
-    main = back[:, : SRC * MAIN].reshape(OWN, SRC, MAIN, 2 * HD).transpose(1, 0, 2, 3)
-    late = back[:, SRC * MAIN :].reshape(OWN, SRC, OVER, 2 * HD).transpose(1, 0, 2, 3)
-    send = jnp.concatenate(
-        [main.reshape(SRC, OWN * MAIN, 2 * HD), late.reshape(SRC, OWN * OVER, 2 * HD)], axis=1
-    )
-    got = lax.all_to_all(send, "dp", split_axis=0, concat_axis=0, tiled=True)
+    weights = gather_weights(out_proj[0])
+    grad_proj, got = owner_work(tokens, weights.reshape(4, OWN, 2, 16, D))
     grad_head, grad_gate = put_back(route_ids, got.reshape(SRC * ROWS, 2 * HD))
     return grad_head.reshape(TOK, TOPK, HD), grad_gate, grad_proj[None]
 
 
 def solution(mesh):
     return jax.shard_map(
-        functools.partial(local, pairs=swap_pairs(mesh)),
+        local,
         mesh=mesh,
         in_specs=(
             P(("dp", "expert"), None, None),

time: 1030 us -> 267 us (0.26)
  the two profiles are of different devices: /device:TPU:6 before, /device:TPU:219 now
where the time goes in v2:
time: 267 us
  Pallas kernels  240 us (90%)
  between operations  14.1 us (5%)
  local copies, waits for them, and re-layouts  11.4 us (4%)
    pallas_call x1, Pallas kernels, owner_work(): pl.pallas_call(owner_kernel, out_shape=(jax.ShapeDtypeStruct((16, D), F32...  158 us
    pallas_call x1, Pallas kernels, gather_weights(): pl.pallas_call(gather_kernel, out_shape=jax.ShapeDtypeStruct((4, 16, 16,...  80.8 us
    unnamed x10, local copies, waits for them, and re-layouts  8.18 us
  transfers between devices with their start and end apart: 1, of which 0 were waited for; matrix products, arithmetic and copies ran while one was open for 1% of the time, Pallas kernels for 30%

profile of v2, /device:TPU:219, one launch (start us, length us, event | category | flops | bytes accessed | tf_op | source)
XLA Modules:
  0.0 266.7 jit_solution(16295560997564801876)
XLA Ops:
  7.2 0.0 all-gather.3.cloned.1.call-start
  7.2 0.7 convert_element_type.3
  7.9 0.1 copy.9
  8.0 0.8 copy.8
  8.8 1.0 copy.15
  9.8 3.1 %concatenate.3 = bf16[128,5248]{1,0:T(8,128)(2,1)} concatenate(bf16[128,4096]{1,0:T(8,128)(2,1)} %param.6, bf16[128,1024]{1,0:T(8,128)(2,1)S(1)} %bitcast.16, bf16[128,8]{1,0:T(8,128)(2,1)S(1)} %copy.8, bf16[128,8]{1,0:T(8,128)(2,1)S(1)} %copy.9, bf16[128,112]{1,0:T(8,128)(2,1)S(1)} %broadcast_in_dim.6), dimensions={1} | concatenate | bytes 2686976 | tf_op jit(solution)/shard_map/concatenate | solution.py:512
  12.9 0.0 all-gather.3.cloned.1.call-update
  12.9 1.4 copy.10.routes_ref
  14.4 80.8 %shard_map.76 = bf16[4,16,16,4096]{3,2,1,0:T(8,128)(2,1)} custom-call(bf16[128,4096]{1,0:T(8,128)(2,1)} %bitcast.15), custom_call_target="tpu_custom_call" | custom-call | bytes 268435456 | tf_op jit(solution)/shard_map/pallas_call | solution.py:206
  95.1 0.0 all-gather.3.cloned.1.call-done
  95.2 158.1 %shard_map.77 = (f32[16,4096]{1,0:T(8,128)}, bf16[8,144,256]{2,1,0:T(8,128)(2,1)}) custom-call(bf16[8,128,5248]{2,1,0:T(8,128)(2,1)} %bitcast.14, bf16[4,8,2,16,4096]{4,3,2,1,0:T(8,128)(2,1)} %bitcast.13), custom_call_target="tpu_custom_call" | custom-call | tf_op jit(solution)/shard_map/pallas_call | solution.py:428
  253.3 0.0 copy-start
  253.3 1.1 copy-done
  254.3 0.0 copy-start.1
  254.3 0.8 copy-done.1
  255.2 1.6 shard_map.78
  256.8 0.8 copy.13
  257.5 0.7 copy.11
  258.2 1.7 copy.17
  (1 shorter events, 0.0 us)
Async XLA Ops:
  7.2 88.0 %all-gather.3.cloned.1.call-start = ((), (), s32[]{:S(2)}) async-start(), calls=%async_computation | async-start | bytes 12091392 | tf_op jit(solution)/shard_map/all_gather | solution.py:522
  253.3 1.1 copy-start
  254.3 0.8 copy-start.1
Sparse Core Ops, SparseCore 0:
  13.1 68.9 all-gather.2

commit v3 on v2

--- a/solution.py
+++ b/solution.py
@@ -20,8 +20,6 @@
 MAIN = 16
 OVER = 2
 ROWS = SRC * (MAIN + OVER)
-META = D + TOPK * HD
-WIDE = META + 128
 STEP = 512
 
 
@@ -29,56 +27,52 @@
     return lax.broadcasted_iota(jnp.int32, shape, axis).astype(F32)
 
 
-def dispatch(base, x_ref, gx, gh, gg, hcat, qm, qo, po, over, arrived):
+def dispatch_source(base, s, xg, xs, gx, gh, gg, hcat, qm, qo, po, over):
     upper = (iota((TOK, TOK), 0) < iota((TOK, TOK), 1)).astype(BF16)
     lane = iota((TOK, 128), 1)
     slot = iota((MAIN, TOK), 0)
-    over[...] = jnp.zeros_like(over)
-
-    def one_source(s, _):
-        arrived(s)
-        meta = x_ref[s, :, META:WIDE].astype(F32)
-        routes = meta.T[TOPK : 2 * TOPK, :]
-        named = [(routes == (base + 2 * j).astype(F32)).astype(F32) for j in range(OWN)]
-        chosen = jnp.concatenate([jnp.sum(n, axis=0, keepdims=True) for n in named], axis=0)
-        before = jnp.dot(chosen.astype(BF16), upper, preferred_element_type=F32)
-        shift = (OVER * s - MAIN).astype(F32)
-        columns = pl.ds(pl.multiple_of(s * TOK, TOK), TOK)
-        picks = []
-        for j in range(OWN):
-            rows = slice(j * MAIN, (j + 1) * MAIN)
-            pos = before[j : j + 1, :]
-            spot = jnp.where(chosen[j : j + 1, :] > 0, pos, -1.0)
-            picks.append((spot == slot).astype(F32))
-            late = jnp.where(spot >= MAIN, spot + shift, -1.0)
-            po[rows, columns] = (late == slot).astype(F32).astype(BF16)
-            own = jnp.where(named[j] > 0, pos, -1.0)
-            own_late = jnp.where(own >= MAIN, own + shift, -1.0)
-            for k in range(TOPK):
-                part = slice(k * TOK, (k + 1) * TOK)
-                qm[rows, part] = (own[k : k + 1, :] == slot).astype(F32).astype(BF16)
-                qo[rows, part] = (own_late[k : k + 1, :] == slot).astype(F32).astype(BF16)
-        pick = jnp.concatenate(picks, axis=0).astype(BF16)
+    meta = xs[s, :, TOPK * HD :].astype(F32)
+    routes = meta.T[TOPK : 2 * TOPK, :]
+    named = [(routes == (base + 2 * j).astype(F32)).astype(F32) for j in range(OWN)]
+    chosen = jnp.concatenate([jnp.sum(n, axis=0, keepdims=True) for n in named], axis=0)
+    before = jnp.dot(chosen.astype(BF16), upper, preferred_element_type=F32)
+    shift = (OVER * s - MAIN).astype(F32)
+    columns = pl.ds(pl.multiple_of(s * TOK, TOK), TOK)
+    picks = []
+    for j in range(OWN):
+        rows = slice(j * MAIN, (j + 1) * MAIN)
+        pos = before[j : j + 1, :]
+        spot = jnp.where(chosen[j : j + 1, :] > 0, pos, -1.0)
+        picks.append((spot == slot).astype(F32))
+        tardy = jnp.where(spot >= MAIN, spot + shift, -1.0)
+        po[rows, columns] = (tardy == slot).astype(F32).astype(BF16)
+        own = jnp.where(named[j] > 0, pos, -1.0)
+        own_tardy = jnp.where(own >= MAIN, own + shift, -1.0)
         for k in range(TOPK):
-            part = slice(k * TOK, (k + 1) * TOK)
-            hcat[part, 0:HD] = x_ref[s, :, D + k * HD : D + (k + 1) * HD]
-            hcat[part, HD : 2 * HD] = jnp.where(lane == k, meta, 0.0).astype(BF16)
-        out_rows = pl.ds(pl.multiple_of(s * MAIN, MAIN), MAIN)
-        for c in range(0, D, STEP):
-            block = jnp.dot(pick, x_ref[s, :, c : c + STEP], preferred_element_type=F32)
-            gx[:, out_rows, c : c + STEP] = block.astype(BF16).reshape(OWN, MAIN, STEP)
-        block = jnp.dot(qm[...], hcat[...], preferred_element_type=F32)
-        gh[:, out_rows, :] = block[:, 0:HD].astype(BF16).reshape(OWN, MAIN, HD)
-        gate = jnp.sum(block[:, HD:], axis=1, keepdims=True)
-        gg[:, out_rows, :] = jnp.broadcast_to(gate, (OWN * MAIN, 128)).reshape(OWN, MAIN, 128)
-        over[...] += jnp.dot(qo[...], hcat[...], preferred_element_type=F32)
-        return 0
-
-    lax.fori_loop(0, SRC, one_source, 0)
+            piece = slice(k * TOK, (k + 1) * TOK)
+            qm[rows, piece] = (own[k : k + 1, :] == slot).astype(F32).astype(BF16)
+            qo[rows, piece] = (own_tardy[k : k + 1, :] == slot).astype(F32).astype(BF16)
+    pick = jnp.concatenate(picks, axis=0).astype(BF16)
+    for k in range(TOPK):
+        piece = slice(k * TOK, (k + 1) * TOK)
+        hcat[piece, 0:HD] = xs[s, :, k * HD : (k + 1) * HD]
+        hcat[piece, HD : 2 * HD] = jnp.where(lane == k, meta, 0.0).astype(BF16)
+    out_rows = pl.ds(pl.multiple_of(s * MAIN, MAIN), MAIN)
+    for c in range(0, D, STEP):
+        block = jnp.dot(pick, xg[s, :, c : c + STEP], preferred_element_type=F32)
+        gx[:, out_rows, c : c + STEP] = block.astype(BF16).reshape(OWN, MAIN, STEP)
+    block = jnp.dot(qm[...], hcat[...], preferred_element_type=F32)
+    gh[:, out_rows, :] = block[:, 0:HD].astype(BF16).reshape(OWN, MAIN, HD)
+    gate = jnp.sum(block[:, HD:], axis=1, keepdims=True)
+    gg[:, out_rows, :] = jnp.broadcast_to(gate, (OWN * MAIN, 128)).reshape(OWN, MAIN, 128)
+    over[...] += jnp.dot(qo[...], hcat[...], preferred_element_type=F32)
+
+
+def dispatch_rest(xg, gx, gh, gg, po, over):
     tail = slice(SRC * MAIN, ROWS)
     width = 2 * 128
     for c in range(0, D, width):
-        tokens = x_ref[:, :, c : c + width].reshape(SRC * TOK, width)
+        tokens = xg[:, :, c : c + width].reshape(SRC * TOK, width)
         block = jnp.dot(po[...], tokens, preferred_element_type=F32)
         gx[:, tail, c : c + width] = block.astype(BF16).reshape(OWN, SRC * OVER, width)
     gh[:, tail, :] = over[:, 0:HD].astype(BF16).reshape(OWN, SRC * OVER, HD)
@@ -122,106 +116,6 @@
         device_id=device,
         device_id_type=MESH,
     )
-
-
-def gather_kernel(proj_ref, w_ref, own, own_sem, keep_sem, zs, zr, ys, yr, fs, fr):
-    dp, y, z, partner, alone = place()
-    at = lambda row, col: (dp, row * 16 + col)
-    ring = lambda v, step, n: lax.rem(v + step + n, n)
-    up, down = at(ring(y, 1, 4), z), at(ring(y, -1, 4), z)
-    right, left = at(y, ring(z, 1, 16)), at(y, ring(z, -1, 16))
-    meet((up, down, right, left), partner, alone)
-
-    mine = proj_ref.at[pl.ds(pl.multiple_of(dp * 16, 16), 16), :]
-    trade = send(mine, own, own_sem.at[0], own_sem.at[1], partner)
-    local = pltpu.make_async_copy(mine, own, own_sem.at[1])
-
-    @pl.when(alone)
-    def _():
-        local.start()
-        local.wait()
-
-    @pl.when(jnp.logical_not(alone))
-    def _():
-        trade.start()
-        trade.wait()
-
-    keep = pltpu.make_async_copy(own, w_ref.at[y, z], keep_sem)
-    keep.start()
-
-    def along_z(src, col, way, hop):
-        return send(src, w_ref.at[y, col], zs.at[way, hop], zr.at[way, hop], (right, left)[way])
-
-    def along_y(src, col, way):
-        return send(src, w_ref.at[y, col], ys.at[way, col], yr.at[way, col], (up, down)[way])
-
-    def spread(src, col):
-        along_y(src, col, 0).start()
-        along_y(src, col, 1).start()
-
-    along_z(own, z, 0, 0).start()
-    along_z(own, z, 1, 0).start()
-    spread(own, z)
-    for hop in range(1, FAR + 1):
-        for way in range(2 if hop < FAR else 1):
-            col = ring(z, -hop if way == 0 else hop, 16)
-            block = w_ref.at[y, col]
-            along_z(block, col, way, hop - 1).wait_recv()
-            if hop < FAR - way:
-                along_z(block, col, way, hop).start()
-            spread(block, col)
-
-    def forward(row, col, way):
-        half = pl.ds(way * HALF, HALF)
-        block = w_ref.at[row, col, :, half]
-        return send(block, block, fs.at[way, col], fr.at[way, col], (up, down)[way])
-
-    below, above, across = ring(y, -1, 4), ring(y, 1, 4), ring(y, 2, 4)
-    order = [0]
-    for hop in range(1, FAR + 1):
-        order += [-hop, hop] if hop < FAR else [-hop]
-    for step in order:
-        col = ring(z, step, 16)
-        send(own, w_ref.at[below, col], ys.at[0, col], yr.at[0, col], up).wait_recv()
-        forward(below, col, 0).start()
-        send(own, w_ref.at[above, col], ys.at[1, col], yr.at[1, col], down).wait_recv()
-        forward(above, col, 1).start()
-    for step in order:
-        col = ring(z, step, 16)
-        forward(across, col, 0).wait_recv()
-        forward(across, col, 1).wait_recv()
-    keep.wait()
-    for hop in range(FAR):
-        for way in range(2):
-            if hop < FAR - way:
-                along_z(own, z, way, hop).wait_send()
-    for col in range(16):
-        for way in range(2):
-            along_y(own, col, way).wait_send()
-            forward(across, col, way).wait_send()
-
-
-def gather_weights(proj):
-    sems = pltpu.SemaphoreType.DMA
-    return pl.pallas_call(
-        gather_kernel,
-        out_shape=jax.ShapeDtypeStruct((4, 16, 16, D), BF16),
-        in_specs=[pl.BlockSpec(memory_space=pl.ANY)],
-        out_specs=pl.BlockSpec(memory_space=pl.ANY),
-        scratch_shapes=[
-            pltpu.VMEM((16, D), BF16),
-            sems((2,)),
-            sems,
-            sems((2, FAR)),
-            sems((2, FAR)),
-            sems((2, 16)),
-            sems((2, 16)),
-            sems((2, 16)),
-            sems((2, 16)),
-        ],
-        compiler_params=pltpu.CompilerParams(collective_id=0, has_side_effects=True),
-        cost_estimate=pl.CostEstimate(flops=0, bytes_accessed=1 << 28, transcendentals=0),
-    )(proj)
 
 
 def expert_step(i, j, wbuf, slot, gx, gh, gg, part, ret, late):
@@ -257,11 +151,14 @@
 
 
 def owner_kernel(
-    x_ref, w_ref, out_ref, got_ref,
-    xbuf, wbuf, gx, gh, gg, hcat, qm, qo, po, over, part, a_in, b_in, comb, zl, zr, zout, ret, late,
-    x_sem, w_sem, ps, pr, cs, cr, zs, zlr, zrr, out_sem, rs, rr, keep_sem,
+    grad_ref, small_ref, proj_ref, out_ref, got_ref, w_ref,
+    xg, xs, own, wbuf, gx, gh, gg, hcat, qm, qo, po, over,
+    part, a_in, b_in, comb, zl, zr, zout, ret, late,
+    mine_sem, ts, tr, own_sem, hold_sem, hs, hr, ys, yr, fs, fr,
+    w_sem, ps, pr, cs, cr, zs, zlr, zrr, out_sem, rs, rr, keep_sem,
 ):
     dp, y, z, partner, alone = place()
+    x, core = dp // 2, lax.rem(dp, 2)
     ring = lambda v, step, n: lax.rem(v + step + n, n)
     yu, yd, y2 = ring(y, 1, 4), ring(y, -1, 4), ring(y, 2, 4)
     up, down = (dp, yu * 16 + z), (dp, yd * 16 + z)
@@ -269,25 +166,163 @@
     here = y * 16 + z
     others = [(lax.rem(dp + k, SRC), here) for k in range(1, SRC)]
     base = (dp // 2) * 16 + lax.rem(dp, 2)
+    low, high = pl.ds(0, HALF), pl.ds(HALF, HALF)
+
+    group = lambda step, flip: 2 * ring(x, step, 4) + (1 - core if flip else core)
+    mine = (
+        pltpu.make_async_copy(grad_ref, xg.at[dp], mine_sem.at[0]),
+        pltpu.make_async_copy(small_ref, xs.at[dp], mine_sem.at[1]),
+    )
+
+    def tokens(n):
+        device = (group((1, -1, 1, -1, 0, 0, 0, 0)[n], n >= 4), here)
+        origin = group((0, 0, -1, 1, 0, -1, 1, 2)[n], False)
+        whole = n in (0, 1, 4, 5, 6, 7)
+        first = n in (0, 1, 4)
+        wide = grad_ref if first else xg.at[origin]
+        narrow = small_ref if first else xs.at[origin]
+        to_wide, to_narrow = xg.at[origin], xs.at[origin]
+        if not whole:
+            half = low if n == 2 else high
+            wide, to_wide = xg.at[origin, :, half], xg.at[origin, :, half]
+        out = [send(wide, to_wide, ts.at[n, 0], tr.at[n, 0], device)]
+        if n != 3:
+            out.append(send(narrow, to_narrow, ts.at[n, 1], tr.at[n, 1], device))
+        return out
+
+    def start(copies):
+        for one in copies:
+            one.start()
+
+    def arrive(copies):
+        for one in copies:
+            one.wait_recv()
+
+    start(mine)
+    meet([up, down, right, left] + others, partner, alone)
+
+    slab = proj_ref.at[pl.ds(pl.multiple_of(dp * 16, 16), 16), :]
+    trade = send(slab, own, own_sem.at[0], own_sem.at[1], partner)
+    local = pltpu.make_async_copy(slab, own, own_sem.at[1])
+
+    @pl.when(alone)
+    def _():
+        local.start()
+
+    @pl.when(jnp.logical_not(alone))
+    def _():
+        trade.start()
+
+    for n in (0, 1, 4):
+        start(tokens(n))
+
+    @pl.when(alone)
+    def _():
+        local.wait()
+
+    @pl.when(jnp.logical_not(alone))
+    def _():
+        trade.wait()
+
+    hold = pltpu.make_async_copy(own, w_ref.at[y, z], hold_sem)
+    hold.start()
+
+    def along_z(src, col, way, hop):
+        return send(src, w_ref.at[y, col], hs.at[way, hop], hr.at[way, hop], (right, left)[way])
+
+    def along_y(src, col, way):
+        return send(src, w_ref.at[y, col], ys.at[way, col], yr.at[way, col], (up, down)[way])
+
+    def forward(row, col, way):
+        block = w_ref.at[row, col, :, (low, high)[way]]
+        return send(block, block, fs.at[way, col], fr.at[way, col], (up, down)[way])
+
+    along_z(own, z, 0, 0).start()
+    along_z(own, z, 1, 0).start()
+    along_y(own, z, 0).start()
+    along_y(own, z, 1).start()
+    for hop in range(1, FAR + 1):
+        for way in range(2 if hop < FAR else 1):
+            col = ring(z, -hop if way == 0 else hop, 16)
+            block = w_ref.at[y, col]
+            along_z(block, col, way, hop - 1).wait_recv()
+            if hop < FAR - way:
+                along_z(block, col, way, hop).start()
+            along_y(block, col, 0).start()
+            along_y(block, col, 1).start()
+
+    def column(step):
+        away = (step + 1) // 2
+        return lax.rem(z + 16 + jnp.where(lax.rem(step, 2) == 1, -away, away), 16)
+
+    def pass_on(step, _):
+        col = column(step)
+        send(own, w_ref.at[yd, col], ys.at[0, col], yr.at[0, col], up).wait_recv()
+        forward(yd, col, 0).start()
+        send(own, w_ref.at[yu, col], ys.at[1, col], yr.at[1, col], down).wait_recv()
+        forward(yu, col, 1).start()
+        return 0
+
+    def settle(step, _):
+        col = column(step)
+        forward(y2, col, 0).wait_recv()
+        forward(y2, col, 1).wait_recv()
+        return 0
 
     def expert_at(i):
         away = 4 - (i + 1) // 2
         return lax.rem(z // 2 + OWN + jnp.where(lax.rem(i, 2) == 1, away, -away), OWN)
 
-    def token_copy(s):
-        return pltpu.make_async_copy(x_ref.at[s], xbuf.at[s], x_sem.at[s])
-
     def weight_copy(i):
         slot = lax.rem(i, 2)
-        return pltpu.make_async_copy(w_ref.at[:, expert_at(i)], wbuf.at[slot], w_sem.at[slot])
-
-    for s in range(SRC):
-        token_copy(s).start()
+        pair = w_ref.at[:, pl.ds(2 * expert_at(i), 2)]
+        return pltpu.make_async_copy(pair, wbuf.at[slot], w_sem.at[slot])
+
+    arrive(tokens(0))
+    start(tokens(2))
+    start(tokens(5))
+    arrive(tokens(1))
+    start(tokens(3))
+    start(tokens(6))
+    for one in mine:
+        one.wait()
+    over[...] = jnp.zeros_like(over)
+
+    def one_source(n, _):
+        @pl.when(n == 1)
+        def _():
+            arrive(tokens(4))
+
+        @pl.when(n == 4)
+        def _():
+            arrive(tokens(5))
+
+        @pl.when(n == 5)
+        def _():
+            arrive(tokens(6))
+
+        @pl.when(n == 6)
+        def _():
+            lax.fori_loop(0, 16, pass_on, 0)
+            arrive(tokens(2))
+            arrive(tokens(3))
+            start(tokens(7))
+
+        @pl.when(n == 7)
+        def _():
+            arrive(tokens(7))
+
+        step = jnp.where(n < 2, 0, jnp.where(n >= 6, 2, jnp.where(lax.rem(n, 2) == 0, -1, 1)))
+        flip = (n == 1) | (n == 4) | (n == 5) | (n == 7)
+        s = 2 * ring(x, step, 4) + jnp.where(flip, 1 - core, core)
+        dispatch_source(base, s, xg, xs, gx, gh, gg, hcat, qm, qo, po, over)
+        return 0
+
+    lax.fori_loop(0, SRC, one_source, 0)
+    dispatch_rest(xg, gx, gh, gg, po, over)
+    lax.fori_loop(0, 16, settle, 0)
+    hold.wait()
     weight_copy(0).start()
-    meet([up, down, right, left] + others, partner, alone)
-    dispatch(base, xbuf, gx, gh, gg, hcat, qm, qo, po, over, lambda s: token_copy(s).wait())
-
-    low, high = pl.ds(0, HALF), pl.ds(HALF, HALF)
 
     def first_sends(i):
         return (
@@ -327,36 +362,42 @@
         total = (
             part[i, y].astype(F32) + b_in[i, 0].astype(F32) + b_in[i, 1].astype(F32)
         )
+        for c in range(2):
+            zout[2 * i + c] = total[16 * c : 16 * (c + 1)]
+
+    def along(i, lagging):
         j = expert_at(i)
         for c in range(2):
             k = 2 * i + c
-            zout[k] = total[16 * c : 16 * (c + 1)]
             ahead = lax.rem(2 * j + c - z + 16, 16)
             behind = lax.rem(16 - ahead, 16)
-
-            @pl.when(ahead < FAR)
+            odd = lax.rem(z, 2) == 1
+            lag = jnp.where(ahead <= FAR, odd, jnp.logical_not(odd)) | (ahead == 0)
+            now = lag if lagging else jnp.logical_not(lag)
+
+            @pl.when(now & (ahead < FAR))
             def _():
                 to_right(k, ahead).wait_recv()
                 zout[k] += zl[ahead]
 
-            @pl.when(behind < FAR - 1)
+            @pl.when(now & (behind < FAR - 1))
             def _():
                 to_left(k, behind).wait_recv()
                 zout[k] += zr[behind]
 
-            @pl.when(jnp.logical_and(ahead >= 1, ahead <= FAR))
+            @pl.when(now & (ahead >= 1) & (ahead <= FAR))
             def _():
                 to_right(k, ahead - 1).start()
 
-            @pl.when(ahead > FAR)
+            @pl.when(now & (ahead > FAR))
             def _():
                 to_left(k, behind - 1).start()
 
-            @pl.when(jnp.logical_and(ahead == 0, alone))
+            @pl.when(now & (ahead == 0) & alone)
             def _():
                 pltpu.make_async_copy(zout.at[k], out_ref, zs.at[k]).start()
 
-            @pl.when(jnp.logical_and(ahead == 0, jnp.logical_not(alone)))
+            @pl.when(now & (ahead == 0) & jnp.logical_not(alone))
             def _():
                 to_partner(k).start()
 
@@ -397,13 +438,18 @@
         def _():
             combine(i - 1)
 
-        @pl.when(i >= 2)
+        @pl.when(jnp.logical_and(i >= 2, i <= OWN + 1))
         def _():
             finish(i - 2)
+            along(i - 2, False)
+
+        @pl.when(i >= 3)
+        def _():
+            along(i - 3, True)
 
         return 0
 
-    lax.fori_loop(0, OWN + 2, one_expert, 0)
+    lax.fori_loop(0, OWN + 3, one_expert, 0)
     for one in returns():
         one.wait()
     keep.wait()
@@ -420,9 +466,24 @@
         return 0
 
     lax.fori_loop(0, OWN, drain, 0)
-
-
-def owner_work(tokens, weights):
+    for n in range(8):
+        for one in tokens(n):
+            one.wait_send()
+    for hop in range(FAR):
+        for way in range(2):
+            if hop < FAR - way:
+                along_z(own, z, way, hop).wait_send()
+
+    def drain_y(col, _):
+        for way in range(2):
+            along_y(own, col, way).wait_send()
+            forward(y2, col, way).wait_send()
+        return 0
+
+    lax.fori_loop(0, 16, drain_y, 0)
+
+
+def owner_work(grads, small, proj):
     sems = pltpu.SemaphoreType.DMA
     vmem = pltpu.VMEM
     return pl.pallas_call(
@@ -430,11 +491,14 @@
         out_shape=(
             jax.ShapeDtypeStruct((16, D), F32),
             jax.ShapeDtypeStruct((SRC, ROWS, 2 * HD), BF16),
+            jax.ShapeDtypeStruct((4, 16, 16, D), BF16),
         ),
-        in_specs=[pl.BlockSpec(memory_space=pl.ANY)] * 2,
-        out_specs=(pl.BlockSpec(memory_space=pl.ANY),) * 2,
+        in_specs=[pl.BlockSpec(memory_space=pl.ANY)] * 3,
+        out_specs=(pl.BlockSpec(memory_space=pl.ANY),) * 3,
         scratch_shapes=[
-            vmem((SRC, TOK, WIDE), BF16),
+            vmem((SRC, TOK, D), BF16),
+            vmem((SRC, TOK, TOPK * HD + 128), BF16),
+            vmem((16, D), BF16),
             vmem((2, 4, 2, 16, D), BF16),
             vmem((OWN, ROWS, D), BF16),
             vmem((OWN, ROWS, HD), BF16),
@@ -453,7 +517,17 @@
             vmem((2 * OWN, 16, D), F32),
             vmem((SRC, ROWS, 2 * HD), BF16),
             vmem((OWN * MAIN, 2 * HD), BF16),
-            sems((SRC,)),
+            sems((2,)),
+            sems((8, 2)),
+            sems((8, 2)),
+            sems((2,)),
+            sems,
+            sems((2, FAR)),
+            sems((2, FAR)),
+            sems((2, 16)),
+            sems((2, 16)),
+            sems((2, 16)),
+            sems((2, 16)),
             sems((2,)),
             sems((OWN, 4)),
             sems((OWN, 4)),
@@ -468,9 +542,9 @@
             sems,
         ],
         compiler_params=pltpu.CompilerParams(
-            collective_id=1, has_side_effects=True, vmem_limit_bytes=67043328
+            collective_id=0, has_side_effects=True, vmem_limit_bytes=67043328
         ),
-    )(tokens, weights)
+    )(grads, small, proj)
 
 
 def return_kernel(routes_ref, back_ref, head_ref, gate_ref):
@@ -509,9 +583,8 @@
 
 
 def local(head_outputs, out_grad, gate_weights, route_ids, out_proj):
-    packed = jnp.concatenate(
+    small = jnp.concatenate(
         [
-            out_grad,
             head_outputs.reshape(TOK, TOPK * HD),
             gate_weights,
             route_ids.astype(BF16),
@@ -519,9 +592,7 @@
         ],
         axis=1,
     )
-    tokens = lax.all_gather(packed, "dp")
-    weights = gather_weights(out_proj[0])
-    grad_proj, got = owner_work(tokens, weights.reshape(4, OWN, 2, 16, D))
+    grad_proj, got, _ = owner_work(out_grad, small, out_proj[0])
     grad_head, grad_gate = put_back(route_ids, got.reshape(SRC * ROWS, 2 * HD))
     return grad_head.reshape(TOK, TOPK, HD), grad_gate, grad_proj[None]
 

time: 267 us -> 231 us (0.87)
  the two profiles are of different devices: /device:TPU:219 before, /device:TPU:6 now
where the time goes in v3:
time: 231 us; the launch traced here: 227 us
  Pallas kernels  218 us (94%)
  local copies, waits for them, and re-layouts  7.7 us (3%)
    pallas_call x1, Pallas kernels, owner_work(): pl.pallas_call(owner_kernel, out_shape=(jax.ShapeDtypeStruct((16, D), F32...  216 us
    unnamed x8, local copies, waits for them, and re-layouts  6.72 us

profile of v3, /device:TPU:6, one launch (start us, length us, event | category | flops | bytes accessed | tf_op | source)
XLA Modules:
  0.0 226.7 jit_solution(3216469253000990115)
XLA Ops:
  0.6 1.0 copy.15
  1.6 0.7 convert_element_type.3
  2.3 0.1 copy.9
  2.4 0.8 copy.8
  3.3 0.9 concatenate.3.small_ref
  4.1 216.0 %shard_map.76 = (f32[16,4096]{1,0:T(8,128)}, bf16[8,144,256]{2,1,0:T(8,128)(2,1)}, bf16[4,16,16,4096]{3,2,1,0:T(8,128)(2,1)}) custom-call(bf16[128,4096]{1,0:T(8,128)(2,1)} %grad_ref.1, bf16[128,1152]{1,0:T(8,128)(2,1)} %concatenate.3.small_ref, bf16[128,4096]{1,0:T(8,128)(2,1)} %bitcast.11), custom_call_target="tpu_custom_call" | custom-call | tf_op jit(solution)/shard_map/pallas_call | solution.py:489
  220.1 0.8 copy.10.routes_ref
  220.9 0.0 copy-start
  220.9 1.1 copy-done
  222.0 1.6 shard_map.77
  223.6 0.8 copy.13
  224.3 0.7 copy.11
  225.0 1.7 copy.17
  (1 shorter events, 0.0 us)
Async XLA Ops:
  220.9 1.1 copy-start

commit v4 on v3

--- a/solution.py
+++ b/solution.py
@@ -82,6 +82,7 @@
 
 MESH = pl.DeviceIdType.MESH
 HALF = D // 2
+ZFIRST = 2816
 FAR = 8
 
 
@@ -154,7 +155,7 @@
     grad_ref, small_ref, proj_ref, out_ref, got_ref, w_ref,
     xg, xs, own, wbuf, gx, gh, gg, hcat, qm, qo, po, over,
     part, a_in, b_in, comb, zl, zr, zout, ret, late,
-    mine_sem, ts, tr, own_sem, hold_sem, hs, hr, ys, yr, fs, fr,
+    mine_sem, ts, tr, own_sem, hold_sem, hs, hr, ys, yr, fs, fr, es, er, bs, br,
     w_sem, ps, pr, cs, cr, zs, zlr, zrr, out_sem, rs, rr, keep_sem,
 ):
     dp, y, z, partner, alone = place()
@@ -227,41 +228,57 @@
     hold = pltpu.make_async_copy(own, w_ref.at[y, z], hold_sem)
     hold.start()
 
+    zcols = pl.ds(0, ZFIRST)
+    ycols = pl.ds(ZFIRST, D - ZFIRST)
+    zhalf = (pl.ds(0, ZFIRST // 2), pl.ds(ZFIRST // 2, ZFIRST // 2))
+    yhalf = (pl.ds(ZFIRST, (D - ZFIRST) // 2), pl.ds((D + ZFIRST) // 2, (D - ZFIRST) // 2))
+
     def along_z(src, col, way, hop):
-        return send(src, w_ref.at[y, col], hs.at[way, hop], hr.at[way, hop], (right, left)[way])
+        to = w_ref.at[y, col, :, zcols]
+        return send(src, to, hs.at[way, hop], hr.at[way, hop], (right, left)[way])
 
     def along_y(src, col, way):
-        return send(src, w_ref.at[y, col], ys.at[way, col], yr.at[way, col], (up, down)[way])
+        to = w_ref.at[y, col, :, zcols]
+        return send(src, to, ys.at[way, col], yr.at[way, col], (up, down)[way])
 
     def forward(row, col, way):
-        block = w_ref.at[row, col, :, (low, high)[way]]
+        block = w_ref.at[row, col, :, zhalf[way]]
         return send(block, block, fs.at[way, col], fr.at[way, col], (up, down)[way])
 
-    along_z(own, z, 0, 0).start()
-    along_z(own, z, 1, 0).start()
-    along_y(own, z, 0).start()
-    along_y(own, z, 1).start()
-    for hop in range(1, FAR + 1):
-        for way in range(2 if hop < FAR else 1):
-            col = ring(z, -hop if way == 0 else hop, 16)
-            block = w_ref.at[y, col]
-            along_z(block, col, way, hop - 1).wait_recv()
-            if hop < FAR - way:
-                along_z(block, col, way, hop).start()
-            along_y(block, col, 0).start()
-            along_y(block, col, 1).start()
+    def early_y(way):
+        to = w_ref.at[y, z, :, ycols]
+        return send(own.at[:, ycols], to, es.at[way], er.at[way], (up, down)[way])
+
+    def early_forward(row, way):
+        block = w_ref.at[row, z, :, yhalf[way]]
+        return send(block, block, es.at[2 + way], er.at[2 + way], (up, down)[way])
+
+    def bundle(col, way, hop):
+        block = w_ref.at[:, col, :, ycols]
+        return send(block, block, bs.at[way, hop], br.at[way, hop], (right, left)[way])
+
+    mine_z = own.at[:, zcols]
+    early_y(0).start()
+    early_y(1).start()
+    along_z(mine_z, z, 0, 0).start()
+    along_z(mine_z, z, 1, 0).start()
+    along_y(mine_z, z, 0).start()
+    along_y(mine_z, z, 1).start()
+    early_y(0).wait_recv()
+    early_forward(yd, 0).start()
+    early_y(1).wait_recv()
+    early_forward(yu, 1).start()
 
     def column(step):
         away = (step + 1) // 2
         return lax.rem(z + 16 + jnp.where(lax.rem(step, 2) == 1, -away, away), 16)
 
-    def pass_on(step, _):
+    def pass_on(step):
         col = column(step)
-        send(own, w_ref.at[yd, col], ys.at[0, col], yr.at[0, col], up).wait_recv()
+        along_y(mine_z, col, 0).wait_recv()
         forward(yd, col, 0).start()
-        send(own, w_ref.at[yu, col], ys.at[1, col], yr.at[1, col], down).wait_recv()
+        along_y(mine_z, col, 1).wait_recv()
         forward(yu, col, 1).start()
-        return 0
 
     def settle(step, _):
         col = column(step)
@@ -269,6 +286,26 @@
         forward(y2, col, 1).wait_recv()
         return 0
 
+    def arrived_z(hop, way):
+        col = ring(z, -hop if way == 0 else hop, 16)
+        block = w_ref.at[y, col, :, zcols]
+        along_z(block, col, way, hop - 1).wait_recv()
+
+        @pl.when(hop < FAR - way)
+        def _():
+            along_z(block, col, way, hop).start()
+
+        along_y(block, col, 0).start()
+        along_y(block, col, 1).start()
+
+    def arrived_bundle(hop, way):
+        col = ring(z, -hop if way == 0 else hop, 16)
+        bundle(col, way, hop - 1).wait_recv()
+
+        @pl.when(hop < FAR - way)
+        def _():
+            bundle(col, way, hop).start()
+
     def expert_at(i):
         away = 4 - (i + 1) // 2
         return lax.rem(z // 2 + OWN + jnp.where(lax.rem(i, 2) == 1, away, -away), OWN)
@@ -278,21 +315,65 @@
         pair = w_ref.at[:, pl.ds(2 * expert_at(i), 2)]
         return pltpu.make_async_copy(pair, wbuf.at[slot], w_sem.at[slot])
 
-    arrive(tokens(0))
-    start(tokens(2))
-    start(tokens(5))
-    arrive(tokens(1))
-    start(tokens(3))
-    start(tokens(6))
-    for one in mine:
-        one.wait()
     over[...] = jnp.zeros_like(over)
 
-    def one_source(n, _):
+    def gather_step(hop, _):
+        @pl.when(hop <= FAR)
+        def _():
+            arrived_z(hop, 0)
+
+        @pl.when(hop < FAR)
+        def _():
+            arrived_z(hop, 1)
+
+        @pl.when(hop == 1)
+        def _():
+            early_forward(y2, 0).wait_recv()
+            early_forward(y2, 1).wait_recv()
+            hold.wait()
+            bundle(z, 0, 0).start()
+            bundle(z, 1, 0).start()
+
+        @pl.when((hop >= 2) & (hop <= FAR + 1))
+        def _():
+            arrived_bundle(hop - 1, 0)
+
+        @pl.when((hop >= 2) & (hop <= FAR))
+        def _():
+            arrived_bundle(hop - 1, 1)
+
+        @pl.when(hop == 2)
+        def _():
+            pass_on(0)
+
+        @pl.when(hop >= 3)
+        def _():
+            pass_on(2 * (hop - 2) - 1)
+
+        @pl.when((hop >= 3) & (hop < FAR + 2))
+        def _():
+            pass_on(2 * (hop - 2))
+
+        n = hop - 3
+
+        @pl.when(n == 0)
+        def _():
+            for one in mine:
+                one.wait()
+
         @pl.when(n == 1)
         def _():
             arrive(tokens(4))
 
+        @pl.when(n == 2)
+        def _():
+            arrive(tokens(0))
+            start(tokens(2))
+            start(tokens(5))
+            arrive(tokens(1))
+            start(tokens(3))
+            start(tokens(6))
+
         @pl.when(n == 4)
         def _():
             arrive(tokens(5))
@@ -303,7 +384,6 @@
 
         @pl.when(n == 6)
         def _():
-            lax.fori_loop(0, 16, pass_on, 0)
             arrive(tokens(2))
             arrive(tokens(3))
             start(tokens(7))
@@ -312,16 +392,21 @@
         def _():
             arrive(tokens(7))
 
-        step = jnp.where(n < 2, 0, jnp.where(n >= 6, 2, jnp.where(lax.rem(n, 2) == 0, -1, 1)))
-        flip = (n == 1) | (n == 4) | (n == 5) | (n == 7)
-        s = 2 * ring(x, step, 4) + jnp.where(flip, 1 - core, core)
-        dispatch_source(base, s, xg, xs, gx, gh, gg, hcat, qm, qo, po, over)
+        @pl.when(n >= 0)
+        def _():
+            step = jnp.where(n < 2, 0, jnp.where(n >= 6, 2, jnp.where(lax.rem(n, 2) == 0, -1, 1)))
+            flip = (n == 1) | (n == 4) | (n == 5) | (n == 7)
+            s = 2 * ring(x, step, 4) + jnp.where(flip, 1 - core, core)
+            dispatch_source(base, s, xg, xs, gx, gh, gg, hcat, qm, qo, po, over)
+
         return 0
 
-    lax.fori_loop(0, SRC, one_source, 0)
-    dispatch_rest(xg, gx, gh, gg, po, over)
-    lax.fori_loop(0, 16, settle, 0)
-    hold.wait()
+    with jax.named_scope("gather"):
+        lax.fori_loop(1, FAR + 3, gather_step, 0)
+    with jax.named_scope("rest"):
+        dispatch_rest(xg, gx, gh, gg, po, over)
+    with jax.named_scope("settle"):
+        lax.fori_loop(0, 16, settle, 0)
     weight_copy(0).start()
 
     def first_sends(i):
@@ -418,7 +503,8 @@
                 weight_copy(i + 1).start()
 
             weight_copy(i).wait()
-            expert_step(i, expert_at(i), wbuf, lax.rem(i, 2), gx, gh, gg, part, ret, late)
+            with jax.named_scope("expert"):
+                expert_step(i, expert_at(i), wbuf, lax.rem(i, 2), gx, gh, gg, part, ret, late)
             for one in first_sends(i):
                 one.start()
 
@@ -436,23 +522,28 @@
 
         @pl.when(jnp.logical_and(i >= 1, i <= OWN))
         def _():
-            combine(i - 1)
+            with jax.named_scope("combine"):
+                combine(i - 1)
 
         @pl.when(jnp.logical_and(i >= 2, i <= OWN + 1))
         def _():
-            finish(i - 2)
-            along(i - 2, False)
+            with jax.named_scope("finish"):
+                finish(i - 2)
+            with jax.named_scope("along"):
+                along(i - 2, False)
 
         @pl.when(i >= 3)
         def _():
-            along(i - 3, True)
+            with jax.named_scope("lagging"):
+                along(i - 3, True)
 
         return 0
 
     lax.fori_loop(0, OWN + 3, one_expert, 0)
-    for one in returns():
-        one.wait()
-    keep.wait()
+    with jax.named_scope("returned"):
+        for one in returns():
+            one.wait()
+        keep.wait()
 
     @pl.when(jnp.logical_not(alone))
     def _():
@@ -472,11 +563,15 @@
     for hop in range(FAR):
         for way in range(2):
             if hop < FAR - way:
-                along_z(own, z, way, hop).wait_send()
+                along_z(mine_z, z, way, hop).wait_send()
+                bundle(z, way, hop).wait_send()
+    for way in range(2):
+        early_y(way).wait_send()
+        early_forward(y2, way).wait_send()
 
     def drain_y(col, _):
         for way in range(2):
-            along_y(own, col, way).wait_send()
+            along_y(mine_z, col, way).wait_send()
             forward(y2, col, way).wait_send()
         return 0
 
@@ -528,6 +623,10 @@
             sems((2, 16)),
             sems((2, 16)),
             sems((2, 16)),
+            sems((4,)),
+            sems((4,)),
+            sems((2, FAR)),
+            sems((2, FAR)),
             sems((2,)),
             sems((OWN, 4)),
             sems((OWN, 4)),

time: 231 us -> 229 us (level); the launches traced: 227 us -> 227 us
  no operation moved by 1% of the time
where the time goes in v4:
time: 229 us; the launch traced here: 227 us
  Pallas kernels  218 us (95%)
  local copies, waits for them, and re-layouts  7.7 us (3%)
    pallas_call x1, Pallas kernels, owner_work(): pl.pallas_call(owner_kernel, out_shape=(jax.ShapeDtypeStruct((16, D), F32...  217 us
    unnamed x8, local copies, waits for them, and re-layouts  6.72 us

profile of v4, /device:TPU:6, one launch (start us, length us, event | category | flops | bytes accessed | tf_op | source)
XLA Modules:
  0.0 227.2 jit_solution(16245578288958514039)
XLA Ops:
  0.6 1.0 copy.15
  1.6 0.7 convert_element_type.3
  2.3 0.1 copy.9
  2.4 0.8 copy.8
  3.3 0.9 concatenate.3.small_ref
  4.1 216.6 %shard_map.76 = (f32[16,4096]{1,0:T(8,128)}, bf16[8,144,256]{2,1,0:T(8,128)(2,1)}, bf16[4,16,16,4096]{3,2,1,0:T(8,128)(2,1)}) custom-call(bf16[128,4096]{1,0:T(8,128)(2,1)} %grad_ref.1, bf16[128,1152]{1,0:T(8,128)(2,1)} %concatenate.3.small_ref, bf16[128,4096]{1,0:T(8,128)(2,1)} %bitcast.11), custom_call_target="tpu_custom_call" | custom-call | tf_op jit(solution)/shard_map/pallas_call | solution.py:584
  220.7 0.8 copy.10.routes_ref
  221.5 0.0 copy-start
  221.5 1.1 copy-done
  222.5 1.6 shard_map.77
  224.2 0.8 copy.13
  224.9 0.7 copy.11
  225.6 1.7 copy.17
  (1 shorter events, 0.0 us)
Async XLA Ops:
  221.5 1.1 copy-start

commit v5 on v4

--- a/solution.py
+++ b/solution.py
@@ -154,7 +154,7 @@
 def owner_kernel(
     grad_ref, small_ref, proj_ref, out_ref, got_ref, w_ref,
     xg, xs, own, wbuf, gx, gh, gg, hcat, qm, qo, po, over,
-    part, a_in, b_in, comb, zl, zr, zout, ret, late,
+    part, a_in, b_in, comb, zl, zr, zout, zsum, ret, late,
     mine_sem, ts, tr, own_sem, hold_sem, hs, hr, ys, yr, fs, fr, es, er, bs, br,
     w_sem, ps, pr, cs, cr, zs, zlr, zrr, out_sem, rs, rr, keep_sem,
 ):
@@ -439,7 +439,10 @@
         return send(zout.at[k], zr.at[slot], zs.at[k], zrr.at[slot], left)
 
     def to_partner(k):
-        return send(zout.at[k], out_ref, zs.at[k], out_sem, partner)
+        return send(zsum.at[k], out_ref, zs.at[k], out_sem, partner)
+
+    def to_self(k):
+        return pltpu.make_async_copy(zsum.at[k], out_ref, zs.at[k])
 
     def finish(i):
         for one in first_sends(i)[2:] + second_sends(i):
@@ -448,7 +451,7 @@
             part[i, y].astype(F32) + b_in[i, 0].astype(F32) + b_in[i, 1].astype(F32)
         )
         for c in range(2):
-            zout[2 * i + c] = total[16 * c : 16 * (c + 1)]
+            zsum[2 * i + c] = total[16 * c : 16 * (c + 1)]
 
     def along(i, lagging):
         j = expert_at(i)
@@ -463,24 +466,26 @@
             @pl.when(now & (ahead < FAR))
             def _():
                 to_right(k, ahead).wait_recv()
-                zout[k] += zl[ahead]
+                zsum[k] += zl[ahead].astype(F32)
 
             @pl.when(now & (behind < FAR - 1))
             def _():
                 to_left(k, behind).wait_recv()
-                zout[k] += zr[behind]
+                zsum[k] += zr[behind].astype(F32)
 
             @pl.when(now & (ahead >= 1) & (ahead <= FAR))
             def _():
+                zout[k] = zsum[k].astype(BF16)
                 to_right(k, ahead - 1).start()
 
             @pl.when(now & (ahead > FAR))
             def _():
+                zout[k] = zsum[k].astype(BF16)
                 to_left(k, behind - 1).start()
 
             @pl.when(now & (ahead == 0) & alone)
             def _():
-                pltpu.make_async_copy(zout.at[k], out_ref, zs.at[k]).start()
+                to_self(k).start()
 
             @pl.when(now & (ahead == 0) & jnp.logical_not(alone))
             def _():
@@ -552,8 +557,22 @@
     def drain(i, _):
         for one in first_sends(i) + second_sends(i):
             one.wait_send()
-        to_right(2 * i, 0).wait_send()
-        to_right(2 * i + 1, 0).wait_send()
+        for c in range(2):
+            k = 2 * i + c
+            last = (i == OWN - 1) & (lax.rem(z, 2) == c)
+
+            @pl.when(jnp.logical_not(last))
+            def _():
+                to_right(k, 0).wait_send()
+
+            @pl.when(last & alone)
+            def _():
+                to_self(k).wait()
+
+            @pl.when(last & jnp.logical_not(alone))
+            def _():
+                to_partner(k).wait_send()
+
         return 0
 
     lax.fori_loop(0, OWN, drain, 0)
@@ -607,8 +626,9 @@
             vmem((OWN, 2, 32, HALF), BF16),
             vmem((OWN, 2, 32, D), BF16),
             vmem((OWN, 2, 32, HALF), BF16),
-            vmem((FAR, 16, D), F32),
-            vmem((FAR - 1, 16, D), F32),
+            vmem((FAR, 16, D), BF16),
+            vmem((FAR - 1, 16, D), BF16),
+            vmem((2 * OWN, 16, D), BF16),
             vmem((2 * OWN, 16, D), F32),
             vmem((SRC, ROWS, 2 * HD), BF16),
             vmem((OWN * MAIN, 2 * HD), BF16),

time: 229 us -> 195 us (0.85)
  Pallas kernels: 218 us -> 186 us
    pallas_call x1, Pallas kernels: 217 us -> 184 us  [owner_work(): pl.pallas_call(owner_kernel, out_shape=(jax.ShapeDtypeStruct((16, D), F32...]
where the time goes in v5:
time: 195 us
  Pallas kernels  186 us (95%)
  local copies, waits for them, and re-layouts  7.7 us (4%)
    pallas_call x1, Pallas kernels, owner_work(): pl.pallas_call(owner_kernel, out_shape=(jax.ShapeDtypeStruct((16, D), F32...  184 us
    unnamed x8, local copies, waits for them, and re-layouts  6.72 us

profile of v5, /device:TPU:6, one launch (start us, length us, event | category | flops | bytes accessed | tf_op | source)
XLA Modules:
  0.0 194.8 jit_solution(3399424155707111756)
XLA Ops:
  0.6 1.0 copy.15
  1.6 0.7 convert_element_type.3
  2.3 0.1 copy.9
  2.4 0.8 copy.8
  3.3 0.9 concatenate.3.small_ref
  4.1 184.1 %shard_map.76 = (f32[16,4096]{1,0:T(8,128)}, bf16[8,144,256]{2,1,0:T(8,128)(2,1)}, bf16[4,16,16,4096]{3,2,1,0:T(8,128)(2,1)}) custom-call(bf16[128,4096]{1,0:T(8,128)(2,1)} %grad_ref.1, bf16[128,1152]{1,0:T(8,128)(2,1)} %concatenate.3.small_ref, bf16[128,4096]{1,0:T(8,128)(2,1)} %bitcast.11), custom_call_target="tpu_custom_call" | custom-call | tf_op jit(solution)/shard_map/pallas_call | solution.py:603
  188.2 0.8 copy.10.routes_ref
  189.0 0.0 copy-start
  189.0 1.1 copy-done
  190.1 1.6 shard_map.77
  191.7 0.8 copy.13
  192.5 0.7 copy.11
  193.1 1.7 copy.17
  (1 shorter events, 0.0 us)
Async XLA Ops:
  189.0 1.1 copy-start

commit v6 on v5

--- a/solution.py
+++ b/solution.py
@@ -82,7 +82,7 @@
 
 MESH = pl.DeviceIdType.MESH
 HALF = D // 2
-ZFIRST = 2816
+ZFIRST = 3584
 FAR = 8
 
 
@@ -510,6 +510,13 @@
             weight_copy(i).wait()
             with jax.named_scope("expert"):
                 expert_step(i, expert_at(i), wbuf, lax.rem(i, 2), gx, gh, gg, part, ret, late)
+        @pl.when(jnp.logical_and(i >= 1, i <= OWN))
+        def _():
+            with jax.named_scope("combine"):
+                combine(i - 1)
+
+        @pl.when(i < OWN)
+        def _():
             for one in first_sends(i):
                 one.start()
 
@@ -524,11 +531,6 @@
             for one in returns():
                 one.start()
             keep.start()
-
-        @pl.when(jnp.logical_and(i >= 1, i <= OWN))
-        def _():
-            with jax.named_scope("combine"):
-                combine(i - 1)
 
         @pl.when(jnp.logical_and(i >= 2, i <= OWN + 1))
         def _():

time: 195 us -> 195 us (level)
  no operation moved by 1% of the time
where the time goes in v6:
time: 195 us; the launch traced here: 194 us
  Pallas kernels  185 us (95%)
  local copies, waits for them, and re-layouts  7.7 us (4%)
    pallas_call x1, Pallas kernels, owner_work(): pl.pallas_call(owner_kernel, out_shape=(jax.ShapeDtypeStruct((16, D), F32...  183 us
    unnamed x8, local copies, waits for them, and re-layouts  6.72 us

profile of v6, /device:TPU:6, one launch (start us, length us, event | category | flops | bytes accessed | tf_op | source)
XLA Modules:
  0.0 193.8 jit_solution(493151291476292104)
XLA Ops:
  0.6 1.0 copy.15
  1.6 0.7 convert_element_type.3
  2.3 0.1 copy.9
  2.4 0.8 copy.8
  3.3 0.9 concatenate.3.small_ref
  4.1 183.1 %shard_map.76 = (f32[16,4096]{1,0:T(8,128)}, bf16[8,144,256]{2,1,0:T(8,128)(2,1)}, bf16[4,16,16,4096]{3,2,1,0:T(8,128)(2,1)}) custom-call(bf16[128,4096]{1,0:T(8,128)(2,1)} %grad_ref.1, bf16[128,1152]{1,0:T(8,128)(2,1)} %concatenate.3.small_ref, bf16[128,4096]{1,0:T(8,128)(2,1)} %bitcast.11), custom_call_target="tpu_custom_call" | custom-call | tf_op jit(solution)/shard_map/pallas_call | solution.py:605
  187.3 0.8 copy.10.routes_ref
  188.1 0.0 copy-start
  188.1 1.1 copy-done
  189.1 1.6 shard_map.77
  190.7 0.8 copy.13
  191.5 0.7 copy.11
  192.1 1.7 copy.17
  (1 shorter events, 0.0 us)
Async XLA Ops:
  188.1 1.1 copy-start
